TPU v7x, 512 devices: a whole 4x4x16 slice. The times are simulated.
512 devices in a mesh: src: 32 (over z, core), tgt: 16 (over y, x).
Axes of the slice: x: 4, y: 4, z: 16, core: 2. Of those that a mesh axis runs over, the one named last changes fastest.
Arguments:
- source: bfloat16 [65536, 1024], P(('src', 'tgt')), may hold values from -16 to 16
- target: bfloat16 [65536, 1024], P(('src', 'tgt')), may hold values from -16 to 16
- src_bucket: int32 [65536], P(('src', 'tgt')), may hold values from 0 to 4095, as said below
- tgt_bucket: int32 [65536], P(('src', 'tgt')), may hold values from 0 to 4095, as said below
- band: int32 [65536], P(('src', 'tgt')), may hold values from 1 to 8, as said below
- route: int32 [65536], P(('src', 'tgt')), may hold values from 0 to 65535, as said below
Outputs:
- src_read: float32 [65536, 1024], P(('src', 'tgt'))
- tgt_read: float32 [65536, 1024], P(('src', 'tgt'))
Inputs may be any that keep to these rules, and one draw needn't show every extreme that they name: `route`: A permutation. Each device's 128 sources go to positions in blocks of devices with the same index along tgt, exactly 4 to each index along src; those from src index s land at offsets s * 4 to (s + 1) * 4 - 1 of the receiving block. `src_bucket`: A source placed by route in the block of device (g, t) has a bucket from g * 128 + t * 8 to g * 128 + (t + 1) * 8 - 1, and each of these 8 buckets occurs among the sources placed in that block. `tgt_bucket`: A target in the block of device (g, t) has a bucket from g * 128 + t * 8 to g * 128 + (t + 1) * 8 - 1, and each of these 8 buckets occurs among that block's targets. Every block of bucket-ordered sources holds a source with band 8.
All inputs are finite; a program needn't handle non-finite values.
Results may differ from a plain program's by a relative error of at most 0.0014.
Values may be sent and summed in bfloat16 or wider, within the bound.
A program may use at most 64 MiB of HBM per device.

v0:
```python
import math

import jax
import jax.numpy as jnp
from jax import lax
from jax.sharding import PartitionSpec as P

lowest = -1e30


def shifted(value, axis, steps):
    count = lax.axis_size(axis)
    pairs = [(source, (source + steps) % count) for source in range(count)]
    return lax.ppermute(value, axis, pairs)


def empty_state(row_count, feature_count):
    return (
        jnp.full((row_count,), lowest, jnp.float32),
        jnp.zeros((row_count,), jnp.float32),
        jnp.zeros((row_count, feature_count), jnp.float32),
    )


def masked_scores(sources, buckets, bands, scaling, visit_rows, visit_bucket):
    scores = (
        lax.dot_general(
            sources, visit_rows, (((1,), (1,)), ((), ())), preferred_element_type=jnp.float32
        )
        * scaling
    )
    allowed = jnp.abs(buckets[:, None] - visit_bucket[None, :]) <= bands[:, None]
    return (jnp.where(allowed, scores, lowest), allowed)


def row_update(row_state, masked, allowed, visit_rows):
    row_max, row_sum, row_read = row_state
    row_new = jnp.maximum(row_max, jnp.max(masked, axis=1))
    weights = jnp.where(allowed, jnp.exp(masked - row_new[:, None]), 0.0)
    row_scale = jnp.exp(row_max - row_new)
    row_sum = row_sum * row_scale + jnp.sum(weights, axis=1)
    row_read = row_read * row_scale[:, None] + jnp.dot(
        weights.astype(jnp.bfloat16), visit_rows, preferred_element_type=jnp.float32
    )
    return (row_new, row_sum, row_read)


def col_update(col_state, masked, allowed, sources):
    col_max, col_sum, col_read = col_state
    col_new = jnp.maximum(col_max, jnp.max(masked, axis=0))
    col_weights = jnp.where(allowed, jnp.exp(masked - col_new[None, :]), 0.0)
    col_scale = jnp.exp(col_max - col_new)
    col_sum = col_sum * col_scale + jnp.sum(col_weights, axis=0)
    col_read = col_read * col_scale[:, None] + lax.dot_general(
        col_weights.astype(jnp.bfloat16),
        sources,
        (((0,), (0,)), ((), ())),
        preferred_element_type=jnp.float32,
    )
    return (col_new, col_sum, col_read)


def encounter(context, row_state, col_state, visit_rows, visit_bucket):
    sources_here, buckets_here, bands_here, scaling = context
    masked, allowed = masked_scores(
        sources_here, buckets_here, bands_here, scaling, visit_rows, visit_bucket
    )
    return (
        row_update(row_state, masked, allowed, visit_rows),
        col_update(col_state, masked, allowed, sources_here),
    )


def on_device(source, target, src_bucket, tgt_bucket, band, route):
    row_count, feature_count = source.shape
    src_count = lax.axis_size("src")
    tgt_count = lax.axis_size("tgt")
    per_peer = row_count // src_count
    dest_slot = route // (row_count * tgt_count) * per_peer + route % per_peer
    placed = jnp.zeros_like(source).at[dest_slot].set(source)
    placed_bucket = jnp.zeros_like(src_bucket).at[dest_slot].set(src_bucket)
    placed_band = jnp.zeros_like(band).at[dest_slot].set(band)
    sources_here, buckets_here, bands_here = (
        lax.all_to_all(placed, "src", split_axis=0, concat_axis=0, tiled=True),
        lax.all_to_all(placed_bucket, "src", split_axis=0, concat_axis=0, tiled=True),
        lax.all_to_all(placed_band, "src", split_axis=0, concat_axis=0, tiled=True),
    )
    scaling = 2.0 / math.sqrt(feature_count)
    context = (sources_here, buckets_here, bands_here, scaling)
    row_state = empty_state(row_count, feature_count)
    col_state = empty_state(row_count, feature_count)
    visit_rows, visit_bucket = (target, tgt_bucket)
    for offset in range(tgt_count):
        row_state, col_state = encounter(context, row_state, col_state, visit_rows, visit_bucket)
        if offset + 1 < tgt_count:
            visit_rows, visit_bucket = shifted((visit_rows, visit_bucket), "tgt", 1)
            col_state = shifted((col_state[0], col_state[1], col_state[2]), "tgt", 1)
        else:
            col_state = shifted((col_state[0], col_state[1], col_state[2]), "tgt", 1)
    src_read = row_state[2] / row_state[1][:, None]
    tgt_read = col_state[2] / col_state[1][:, None]
    return (src_read, tgt_read)


def solution(mesh):
    placed = (
        P(("src", "tgt"), None),
        P(("src", "tgt"), None),
        P(("src", "tgt")),
        P(("src", "tgt")),
        P(("src", "tgt")),
        P(("src", "tgt")),
    )
    return jax.shard_map(
        on_device,
        mesh=mesh,
        in_specs=placed,
        out_specs=(P(("src", "tgt"), None), P(("src", "tgt"), None)),
        check_vma=False,
    )
```

profile of v0, /device:TPU:32, one launch (start us, length us, event | category | flops | bytes accessed | tf_op | source)
XLA Modules:
  0.0 651.2 jit_solution(8987389445520533225)
XLA Ops:
  0.6 3.4 collective-permute-start.1
  4.0 10.2 %collective-permute-done.1 = bf16[128,1024]{1,0:T(8,128)(2,1)S(1)} collective-permute-done((bf16[128,1024]{1,0:T(8,128)(2,1)}, bf16[128,1024]{1,0:T(8,128)(2,1)S(1)}, u32[]{:S(2)}, u32[]{:S(2)}) %collective-permute-start.1) | collective-permute-done | bytes 262176 | tf_op jit(solution)/shard_map/ppermute | solution.py:14
  16.2 10.6 %collective-permute-done.3 = bf16[128,1024]{1,0:T(8,128)(2,1)S(1)} collective-permute-done((bf16[128,1024]{1,0:T(8,128)(2,1)S(1)}, bf16[128,1024]{1,0:T(8,128)(2,1)S(1)}, u32[]{:S(2)}, u32[]{:S(2)}) %collective-permute-start.3) | collective-permute-done | bytes 262176 | tf_op jit(solution)/shard_map/ppermute | solution.py:14
  28.7 9.7 %collective-permute-done.5 = bf16[128,1024]{1,0:T(8,128)(2,1)S(1)} collective-permute-done((bf16[128,1024]{1,0:T(8,128)(2,1)S(1)}, bf16[128,1024]{1,0:T(8,128)(2,1)S(1)}, u32[]{:S(2)}, u32[]{:S(2)}) %collective-permute-start.5) | collective-permute-done | bytes 262176 | tf_op jit(solution)/shard_map/ppermute | solution.py:14
  42.9 15.4 %all-to-all-start = ((s32[32,4,1]{1,2,0:T(1,128)}), s32[32,4,1]{1,2,0:T(1,128)S(1)}, u32[]{:S(2)}, u32[]{:S(2)}) async-start(s32[32,4,1]{1,2,0:T(1,128)} %bitcast), calls=%async_computation | async-start | bytes 32768 | tf_op jit(solution)/shard_map/all_to_all | solution.py:85
  60.0 9.3 %all-to-all-done = s32[32,4,1]{1,2,0:T(1,128)S(1)} async-done(((s32[32,4,1]{1,2,0:T(1,128)}), s32[32,4,1]{1,2,0:T(1,128)S(1)}, u32[]{:S(2)}, u32[]{:S(2)}) %all-to-all-start) | async-done | bytes 544 | tf_op jit(solution)/shard_map/all_to_all | solution.py:85
  69.4 4.9 all-to-all-start.1
  76.8 8.8 %all-to-all-done.1 = s32[32,4,1]{1,2,0:T(1,128)S(1)} async-done(((s32[32,4,1]{1,2,0:T(1,128)}), s32[32,4,1]{1,2,0:T(1,128)S(1)}, u32[]{:S(2)}, u32[]{:S(2)}) %all-to-all-start.1) | async-done | bytes 544 | tf_op jit(solution)/shard_map/all_to_all | solution.py:86
  85.6 5.0 all-to-all-start.2
  92.5 11.9 %collective-permute-done.9 = bf16[128,1024]{1,0:T(8,128)(2,1)S(1)} collective-permute-done((bf16[128,1024]{1,0:T(8,128)(2,1)S(1)}, bf16[128,1024]{1,0:T(8,128)(2,1)S(1)}, u32[]{:S(2)}, u32[]{:S(2)}) %collective-permute-start.9) | collective-permute-done | bytes 262176 | tf_op jit(solution)/shard_map/ppermute | solution.py:14
  106.3 11.1 %collective-permute-done.11 = bf16[128,1024]{1,0:T(8,128)(2,1)S(1)} collective-permute-done((bf16[128,1024]{1,0:T(8,128)(2,1)S(1)}, bf16[128,1024]{1,0:T(8,128)(2,1)S(1)}, u32[]{:S(2)}, u32[]{:S(2)}) %collective-permute-start.11) | collective-permute-done | bytes 262176 | tf_op jit(solution)/shard_map/ppermute | solution.py:14
  119.4 1.9 collective-permute-start
  121.3 8.4 %collective-permute-done = s32[128]{0:T(128)S(1)} collective-permute-done((s32[128]{0:T(128)S(1)}, s32[128]{0:T(128)S(1)}, u32[]{:S(2)}, u32[]{:S(2)}) %collective-permute-start) | collective-permute-done | bytes 544 | tf_op jit(solution)/shard_map/ppermute | solution.py:14
  131.6 6.8 %collective-permute-done.2 = s32[128]{0:T(128)S(1)} collective-permute-done((s32[128]{0:T(128)S(1)}, s32[128]{0:T(128)S(1)}, u32[]{:S(2)}, u32[]{:S(2)}) %collective-permute-start.2) | collective-permute-done | bytes 544 | tf_op jit(solution)/shard_map/ppermute | solution.py:14
  140.3 6.8 %collective-permute-done.4 = s32[128]{0:T(128)S(1)} collective-permute-done((s32[128]{0:T(128)S(1)}, s32[128]{0:T(128)S(1)}, u32[]{:S(2)}, u32[]{:S(2)}) %collective-permute-start.4) | collective-permute-done | bytes 544 | tf_op jit(solution)/shard_map/ppermute | solution.py:14
  149.1 6.8 %collective-permute-done.6 = s32[128]{0:T(128)S(1)} collective-permute-done((s32[128]{0:T(128)S(1)}, s32[128]{0:T(128)S(1)}, u32[]{:S(2)}, u32[]{:S(2)}) %collective-permute-start.6) | collective-permute-done | bytes 544 | tf_op jit(solution)/shard_map/ppermute | solution.py:14
  157.8 6.8 %collective-permute-done.8 = s32[128]{0:T(128)S(1)} collective-permute-done((s32[128]{0:T(128)S(1)}, s32[128]{0:T(128)S(1)}, u32[]{:S(2)}, u32[]{:S(2)}) %collective-permute-start.8) | collective-permute-done | bytes 544 | tf_op jit(solution)/shard_map/ppermute | solution.py:14
  166.6 6.8 %collective-permute-done.10 = s32[128]{0:T(128)S(1)} collective-permute-done((s32[128]{0:T(128)S(1)}, s32[128]{0:T(128)S(1)}, u32[]{:S(2)}, u32[]{:S(2)}) %collective-permute-start.10) | collective-permute-done | bytes 544 | tf_op jit(solution)/shard_map/ppermute | solution.py:14
  175.3 6.8 %collective-permute-done.12 = s32[128]{0:T(128)S(1)} collective-permute-done((s32[128]{0:T(128)S(1)}, s32[128]{0:T(128)S(1)}, u32[]{:S(2)}, u32[]{:S(2)}) %collective-permute-start.12) | collective-permute-done | bytes 544 | tf_op jit(solution)/shard_map/ppermute | solution.py:14
  184.1 6.8 %collective-permute-done.14 = s32[128]{0:T(128)S(1)} collective-permute-done((s32[128]{0:T(128)S(1)}, s32[128]{0:T(128)S(1)}, u32[]{:S(2)}, u32[]{:S(2)}) %collective-permute-start.14) | collective-permute-done | bytes 544 | tf_op jit(solution)/shard_map/ppermute | solution.py:14
  192.8 6.8 %collective-permute-done.16 = s32[128]{0:T(128)S(1)} collective-permute-done((s32[128]{0:T(128)S(1)}, s32[128]{0:T(128)S(1)}, u32[]{:S(2)}, u32[]{:S(2)}) %collective-permute-start.16) | collective-permute-done | bytes 544 | tf_op jit(solution)/shard_map/ppermute | solution.py:14
  201.6 6.8 %collective-permute-done.18 = s32[128]{0:T(128)S(1)} collective-permute-done((s32[128]{0:T(128)S(1)}, s32[128]{0:T(128)S(1)}, u32[]{:S(2)}, u32[]{:S(2)}) %collective-permute-start.18) | collective-permute-done | bytes 544 | tf_op jit(solution)/shard_map/ppermute | solution.py:14
  210.3 6.8 %collective-permute-done.20 = s32[128]{0:T(128)S(1)} collective-permute-done((s32[128]{0:T(128)S(1)}, s32[128]{0:T(128)S(1)}, u32[]{:S(2)}, u32[]{:S(2)}) %collective-permute-start.20) | collective-permute-done | bytes 544 | tf_op jit(solution)/shard_map/ppermute | solution.py:14
  219.0 6.8 %collective-permute-done.22 = s32[128]{0:T(128)S(1)} collective-permute-done((s32[128]{0:T(128)S(1)}, s32[128]{0:T(128)S(1)}, u32[]{:S(2)}, u32[]{:S(2)}) %collective-permute-start.22) | collective-permute-done | bytes 544 | tf_op jit(solution)/shard_map/ppermute | solution.py:14
  227.8 6.8 %collective-permute-done.24 = s32[128]{0:T(128)S(1)} collective-permute-done((s32[128]{0:T(128)S(1)}, s32[128]{0:T(128)S(1)}, u32[]{:S(2)}, u32[]{:S(2)}) %collective-permute-start.24) | collective-permute-done | bytes 544 | tf_op jit(solution)/shard_map/ppermute | solution.py:14
  238.7 4.7 collective-permute-done.26
  245.4 1.9 collective-permute-start.15
  247.6 1.9 collective-permute-start.31
  249.5 7.4 %collective-permute-done.15 = bf16[128,1024]{1,0:T(8,128)(2,1)S(1)} collective-permute-done((bf16[128,1024]{1,0:T(8,128)(2,1)S(1)}, bf16[128,1024]{1,0:T(8,128)(2,1)S(1)}, u32[]{:S(2)}, u32[]{:S(2)}) %collective-permute-start.15) | collective-permute-done | bytes 262176 | tf_op jit(solution)/shard_map/ppermute | solution.py:14
  261.4 7.1 %collective-permute-done.33 = f32[128]{0:T(128)S(1)} collective-permute-done((f32[128]{0:T(128)S(1)}, f32[128]{0:T(128)S(1)}, u32[]{:S(2)}, u32[]{:S(2)}) %collective-permute-start.33) | collective-permute-done | bytes 544 | tf_op jit(solution)/shard_map/ppermute | solution.py:14
  270.5 1.9 collective-permute-start.19
  272.8 4.6 collective-permute-done.35
  279.6 6.5 collective-permute-done.37
  290.2 4.6 collective-permute-done.39
  297.1 6.5 collective-permute-done.41
  307.7 4.6 collective-permute-done.43
  314.6 6.5 collective-permute-done.45
  323.0 1.9 collective-permute-start.25
  325.2 4.6 collective-permute-done.47
  332.1 6.5 collective-permute-done.49
  340.5 1.9 collective-permute-start.27
  342.7 4.6 collective-permute-done.51
  349.6 6.5 collective-permute-done.53
  360.2 4.6 collective-permute-done.55
  367.0 6.6 %collective-permute-done.57 = f32[128]{0:T(128)S(1)} collective-permute-done((f32[128]{0:T(128)S(1)}, f32[128]{0:T(128)S(1)}, u32[]{:S(2)}, u32[]{:S(2)}) %collective-permute-start.57) | collective-permute-done | bytes 544 | tf_op jit(solution)/shard_map/ppermute | solution.py:14
  375.9 6.4 collective-permute-done.59
  383.0 1.9 collective-permute-start.30
  387.2 10.3 %collective-permute-done.61 = f32[128]{0:T(128)S(1)} collective-permute-done((f32[128]{0:T(128)S(1)}, f32[128]{0:T(128)S(1)}, u32[]{:S(2)}, u32[]{:S(2)}) %collective-permute-start.61) | collective-permute-done | bytes 544 | tf_op jit(solution)/shard_map/ppermute | solution.py:14
  402.0 10.3 %collective-permute-done.62 = f32[128]{0:T(128)S(1)} collective-permute-done((f32[128]{0:T(128)S(1)}, f32[128]{0:T(128)S(1)}, u32[]{:S(2)}, u32[]{:S(2)}) %collective-permute-start.62) | collective-permute-done | bytes 544 | tf_op jit(solution)/shard_map/ppermute | solution.py:14
  416.8 11.4 %collective-permute-done.63 = f32[128]{0:T(128)S(1)} collective-permute-done((f32[128]{0:T(128)S(1)}, f32[128]{0:T(128)S(1)}, u32[]{:S(2)}, u32[]{:S(2)}) %collective-permute-start.63) | collective-permute-done | bytes 544 | tf_op jit(solution)/shard_map/ppermute | solution.py:14
  428.5 2.1 collective-permute-start.36
  432.6 12.9 %collective-permute-done.64 = f32[128]{0:T(128)S(1)} collective-permute-done((f32[128]{0:T(128)S(1)}, f32[128]{0:T(128)S(1)}, u32[]{:S(2)}, u32[]{:S(2)}) %collective-permute-start.64) | collective-permute-done | bytes 544 | tf_op jit(solution)/shard_map/ppermute | solution.py:14
  449.7 14.0 %collective-permute-done.65 = f32[128]{0:T(128)S(1)} collective-permute-done((f32[128]{0:T(128)S(1)}, f32[128]{0:T(128)S(1)}, u32[]{:S(2)}, u32[]{:S(2)}) %collective-permute-start.65) | collective-permute-done | bytes 544 | tf_op jit(solution)/shard_map/ppermute | solution.py:14
  468.0 15.2 %collective-permute-done.66 = f32[128]{0:T(128)S(1)} collective-permute-done((f32[128]{0:T(128)S(1)}, f32[128]{0:T(128)S(1)}, u32[]{:S(2)}, u32[]{:S(2)}) %collective-permute-start.66) | collective-permute-done | bytes 544 | tf_op jit(solution)/shard_map/ppermute | solution.py:14
  487.3 16.1 %collective-permute-done.67 = f32[128]{0:T(128)S(1)} collective-permute-done((f32[128]{0:T(128)S(1)}, f32[128]{0:T(128)S(1)}, u32[]{:S(2)}, u32[]{:S(2)}) %collective-permute-start.67) | collective-permute-done | bytes 544 | tf_op jit(solution)/shard_map/ppermute | solution.py:14
  507.7 15.2 %collective-permute-done.68 = f32[128]{0:T(128)S(1)} collective-permute-done((f32[128]{0:T(128)S(1)}, f32[128]{0:T(128)S(1)}, u32[]{:S(2)}, u32[]{:S(2)}) %collective-permute-start.68) | collective-permute-done | bytes 544 | tf_op jit(solution)/shard_map/ppermute | solution.py:14
  527.5 13.9 %collective-permute-done.69 = f32[128]{0:T(128)S(1)} collective-permute-done((f32[128]{0:T(128)S(1)}, f32[128]{0:T(128)S(1)}, u32[]{:S(2)}, u32[]{:S(2)}) %collective-permute-start.69) | collective-permute-done | bytes 544 | tf_op jit(solution)/shard_map/ppermute | solution.py:14
  546.2 12.7 %collective-permute-done.70 = f32[128]{0:T(128)S(1)} collective-permute-done((f32[128]{0:T(128)S(1)}, f32[128]{0:T(128)S(1)}, u32[]{:S(2)}, u32[]{:S(2)}) %collective-permute-start.70) | collective-permute-done | bytes 544 | tf_op jit(solution)/shard_map/ppermute | solution.py:14
  563.8 11.7 %collective-permute-done.71 = f32[128]{0:T(128)S(1)} collective-permute-done((f32[128]{0:T(128)S(1)}, f32[128]{0:T(128)S(1)}, u32[]{:S(2)}, u32[]{:S(2)}) %collective-permute-start.71) | collective-permute-done | bytes 544 | tf_op jit(solution)/shard_map/ppermute | solution.py:14
  580.3 10.7 %collective-permute-done.72 = f32[128]{0:T(128)S(1)} collective-permute-done((f32[128]{0:T(128)S(1)}, f32[128]{0:T(128)S(1)}, u32[]{:S(2)}, u32[]{:S(2)}) %collective-permute-start.72) | collective-permute-done | bytes 544 | tf_op jit(solution)/shard_map/ppermute | solution.py:14
  595.8 10.0 %collective-permute-done.73 = f32[128]{0:T(128)S(1)} collective-permute-done((f32[128]{0:T(128)S(1)}, f32[128]{0:T(128)S(1)}, u32[]{:S(2)}, u32[]{:S(2)}) %collective-permute-start.73) | collective-permute-done | bytes 544 | tf_op jit(solution)/shard_map/ppermute | solution.py:14
  610.6 10.0 %collective-permute-done.74 = f32[128]{0:T(128)S(1)} collective-permute-done((f32[128]{0:T(128)S(1)}, f32[128]{0:T(128)S(1)}, u32[]{:S(2)}, u32[]{:S(2)}) %collective-permute-start.74) | collective-permute-done | bytes 544 | tf_op jit(solution)/shard_map/ppermute | solution.py:14
  625.5 10.0 %collective-permute-done.75 = f32[128]{0:T(128)S(1)} collective-permute-done((f32[128]{0:T(128)S(1)}, f32[128]{0:T(128)S(1)}, u32[]{:S(2)}, u32[]{:S(2)}) %collective-permute-start.75) | collective-permute-done | bytes 544 | tf_op jit(solution)/shard_map/ppermute | solution.py:14
  641.4 8.9 %collective-permute-done.76 = f32[128]{0:T(128)S(1)} collective-permute-done((f32[128]{0:T(128)S(1)}, f32[128]{0:T(128)S(1)}, u32[]{:S(2)}, u32[]{:S(2)}) %collective-permute-start.76) | collective-permute-done | bytes 544 | tf_op jit(solution)/shard_map/ppermute | solution.py:14
  (200 shorter events, 157.6 us)
Async XLA Ops:
  0.6 13.6 %collective-permute-start.1 = (bf16[128,1024]{1,0:T(8,128)(2,1)}, bf16[128,1024]{1,0:T(8,128)(2,1)S(1)}, u32[]{:S(2)}, u32[]{:S(2)}) collective-permute-start(bf16[128,1024]{1,0:T(8,128)(2,1)} %param.7), channel_id=1, source_target_pairs={{0,1},{1,2},{2,3},{3,4},{4,5},{5,6},{6,7},{7,8},{8,9},{9,10},{10,1... | collective-permute-start | bytes 786440 | tf_op jit(solution)/shard_map/ppermute | solution.py:14
  14.3 12.6 %collective-permute-start.3 = (bf16[128,1024]{1,0:T(8,128)(2,1)S(1)}, bf16[128,1024]{1,0:T(8,128)(2,1)S(1)}, u32[]{:S(2)}, u32[]{:S(2)}) collective-permute-start(bf16[128,1024]{1,0:T(8,128)(2,1)S(1)} %collective-permute-done.1), channel_id=1, source_target_pairs={{0,1},{1,2},{2,3},{3,4},{4,5},{5,6},{6,7},{7,8},{8,9},{9,10},{10,1... | collective-permute-start | bytes 786440 | tf_op jit(solution)/shard_map/ppermute | solution.py:14
  26.8 11.6 %collective-permute-start.5 = (bf16[128,1024]{1,0:T(8,128)(2,1)S(1)}, bf16[128,1024]{1,0:T(8,128)(2,1)S(1)}, u32[]{:S(2)}, u32[]{:S(2)}) collective-permute-start(bf16[128,1024]{1,0:T(8,128)(2,1)S(1)} %collective-permute-done.3), channel_id=1, source_target_pairs={{0,1},{1,2},{2,3},{3,4},{4,5},{5,6},{6,7},{7,8},{8,9},{9,10},{10,1... | collective-permute-start | bytes 786440 | tf_op jit(solution)/shard_map/ppermute | solution.py:14
  38.4 52.1 %collective-permute-start.7 = (bf16[128,1024]{1,0:T(8,128)(2,1)S(1)}, bf16[128,1024]{1,0:T(8,128)(2,1)S(1)}, u32[]{:S(2)}, u32[]{:S(2)}) collective-permute-start(bf16[128,1024]{1,0:T(8,128)(2,1)S(1)} %collective-permute-done.5), channel_id=1, source_target_pairs={{0,1},{1,2},{2,3},{3,4},{4,5},{5,6},{6,7},{7,8},{8,9},{9,10},{10,1... | collective-permute-start | bytes 786440 | tf_op jit(solution)/shard_map/ppermute | solution.py:14
  42.9 26.5 %all-to-all-start = ((s32[32,4,1]{1,2,0:T(1,128)}), s32[32,4,1]{1,2,0:T(1,128)S(1)}, u32[]{:S(2)}, u32[]{:S(2)}) async-start(s32[32,4,1]{1,2,0:T(1,128)} %bitcast), calls=%async_computation | async-start | bytes 32768 | tf_op jit(solution)/shard_map/all_to_all | solution.py:85
  69.4 16.2 %all-to-all-start.1 = ((s32[32,4,1]{1,2,0:T(1,128)}), s32[32,4,1]{1,2,0:T(1,128)S(1)}, u32[]{:S(2)}, u32[]{:S(2)}) async-start(s32[32,4,1]{1,2,0:T(1,128)} %bitcast.1), calls=%async_computation.1 | async-start | bytes 32768 | tf_op jit(solution)/shard_map/all_to_all | solution.py:86
  85.6 159.7 %all-to-all-start.2 = ((bf16[32,4,1024]{2,1,0:T(4,128)(2,1)}), bf16[32,4,1024]{2,1,0:T(4,128)(2,1)S(1)}, u32[]{:S(2)}, u32[]{:S(2)}) async-start(bf16[32,4,1024]{2,1,0:T(4,128)(2,1)} %all_to_all.24), calls=%async_computation.2 | async-start | bytes 524288 | tf_op jit(solution)/shard_map/all_to_all | solution.py:84
  90.6 13.9 %collective-permute-start.9 = (bf16[128,1024]{1,0:T(8,128)(2,1)S(1)}, bf16[128,1024]{1,0:T(8,128)(2,1)S(1)}, u32[]{:S(2)}, u32[]{:S(2)}) collective-permute-start(bf16[128,1024]{1,0:T(8,128)(2,1)S(1)} %collective-permute-done.7), channel_id=1, source_target_pairs={{0,1},{1,2},{2,3},{3,4},{4,5},{5,6},{6,7},{7,8},{8,9},{9,10},{10,1... | collective-permute-start | bytes 786440 | tf_op jit(solution)/shard_map/ppermute | solution.py:14
  104.4 13.1 %collective-permute-start.11 = (bf16[128,1024]{1,0:T(8,128)(2,1)S(1)}, bf16[128,1024]{1,0:T(8,128)(2,1)S(1)}, u32[]{:S(2)}, u32[]{:S(2)}) collective-permute-start(bf16[128,1024]{1,0:T(8,128)(2,1)S(1)} %collective-permute-done.9), channel_id=1, source_target_pairs={{0,1},{1,2},{2,3},{3,4},{4,5},{5,6},{6,7},{7,8},{8,9},{9,10},{10,1... | collective-permute-start | bytes 786440 | tf_op jit(solution)/shard_map/ppermute | solution.py:14
  117.5 127.9 %collective-permute-start.13 = (bf16[128,1024]{1,0:T(8,128)(2,1)S(1)}, bf16[128,1024]{1,0:T(8,128)(2,1)S(1)}, u32[]{:S(2)}, u32[]{:S(2)}) collective-permute-start(bf16[128,1024]{1,0:T(8,128)(2,1)S(1)} %collective-permute-done.11), channel_id=1, source_target_pairs={{0,1},{1,2},{2,3},{3,4},{4,5},{5,6},{6,7},{7,8},{8,9},{9,10},{10,1... | collective-permute-start | bytes 786440 | tf_op jit(solution)/shard_map/ppermute | solution.py:14
  119.4 10.3 %collective-permute-start = (s32[128]{0:T(128)S(1)}, s32[128]{0:T(128)S(1)}, u32[]{:S(2)}, u32[]{:S(2)}) collective-permute-start(s32[128]{0:T(128)S(1)} %copy-done.1), channel_id=1, source_target_pairs={{0,1},{1,2},{2,3},{3,4},{4,5},{5,6},{6,7},{7,8},{8,9},{9,10},{10,1... | collective-permute-start | bytes 1544 | tf_op jit(solution)/shard_map/ppermute | solution.py:14
  129.7 8.7 %collective-permute-start.2 = (s32[128]{0:T(128)S(1)}, s32[128]{0:T(128)S(1)}, u32[]{:S(2)}, u32[]{:S(2)}) collective-permute-start(s32[128]{0:T(128)S(1)} %collective-permute-done), channel_id=1, source_target_pairs={{0,1},{1,2},{2,3},{3,4},{4,5},{5,6},{6,7},{7,8},{8,9},{9,10},{10,1... | collective-permute-start | bytes 1544 | tf_op jit(solution)/shard_map/ppermute | solution.py:14
  138.4 8.7 %collective-permute-start.4 = (s32[128]{0:T(128)S(1)}, s32[128]{0:T(128)S(1)}, u32[]{:S(2)}, u32[]{:S(2)}) collective-permute-start(s32[128]{0:T(128)S(1)} %collective-permute-done.2), channel_id=1, source_target_pairs={{0,1},{1,2},{2,3},{3,4},{4,5},{5,6},{6,7},{7,8},{8,9},{9,10},{10,1... | collective-permute-start | bytes 1544 | tf_op jit(solution)/shard_map/ppermute | solution.py:14
  147.2 8.7 %collective-permute-start.6 = (s32[128]{0:T(128)S(1)}, s32[128]{0:T(128)S(1)}, u32[]{:S(2)}, u32[]{:S(2)}) collective-permute-start(s32[128]{0:T(128)S(1)} %collective-permute-done.4), channel_id=1, source_target_pairs={{0,1},{1,2},{2,3},{3,4},{4,5},{5,6},{6,7},{7,8},{8,9},{9,10},{10,1... | collective-permute-start | bytes 1544 | tf_op jit(solution)/shard_map/ppermute | solution.py:14
  155.9 8.7 %collective-permute-start.8 = (s32[128]{0:T(128)S(1)}, s32[128]{0:T(128)S(1)}, u32[]{:S(2)}, u32[]{:S(2)}) collective-permute-start(s32[128]{0:T(128)S(1)} %collective-permute-done.6), channel_id=1, source_target_pairs={{0,1},{1,2},{2,3},{3,4},{4,5},{5,6},{6,7},{7,8},{8,9},{9,10},{10,1... | collective-permute-start | bytes 1544 | tf_op jit(solution)/shard_map/ppermute | solution.py:14
  164.7 8.7 %collective-permute-start.10 = (s32[128]{0:T(128)S(1)}, s32[128]{0:T(128)S(1)}, u32[]{:S(2)}, u32[]{:S(2)}) collective-permute-start(s32[128]{0:T(128)S(1)} %collective-permute-done.8), channel_id=1, source_target_pairs={{0,1},{1,2},{2,3},{3,4},{4,5},{5,6},{6,7},{7,8},{8,9},{9,10},{10,1... | collective-permute-start | bytes 1544 | tf_op jit(solution)/shard_map/ppermute | solution.py:14
  173.4 8.7 %collective-permute-start.12 = (s32[128]{0:T(128)S(1)}, s32[128]{0:T(128)S(1)}, u32[]{:S(2)}, u32[]{:S(2)}) collective-permute-start(s32[128]{0:T(128)S(1)} %collective-permute-done.10), channel_id=1, source_target_pairs={{0,1},{1,2},{2,3},{3,4},{4,5},{5,6},{6,7},{7,8},{8,9},{9,10},{10,1... | collective-permute-start | bytes 1544 | tf_op jit(solution)/shard_map/ppermute | solution.py:14
  217.1 8.7 %collective-permute-start.22 = (s32[128]{0:T(128)S(1)}, s32[128]{0:T(128)S(1)}, u32[]{:S(2)}, u32[]{:S(2)}) collective-permute-start(s32[128]{0:T(128)S(1)} %collective-permute-done.20), channel_id=1, source_target_pairs={{0,1},{1,2},{2,3},{3,4},{4,5},{5,6},{6,7},{7,8},{8,9},{9,10},{10,1... | collective-permute-start | bytes 1544 | tf_op jit(solution)/shard_map/ppermute | solution.py:14
  225.9 8.7 %collective-permute-start.24 = (s32[128]{0:T(128)S(1)}, s32[128]{0:T(128)S(1)}, u32[]{:S(2)}, u32[]{:S(2)}) collective-permute-start(s32[128]{0:T(128)S(1)} %collective-permute-done.22), channel_id=1, source_target_pairs={{0,1},{1,2},{2,3},{3,4},{4,5},{5,6},{6,7},{7,8},{8,9},{9,10},{10,1... | collective-permute-start | bytes 1544 | tf_op jit(solution)/shard_map/ppermute | solution.py:14
  243.3 132.2 %collective-permute-start.28 = (s32[128]{0:T(128)S(1)}, s32[128]{0:T(128)S(1)}, u32[]{:S(2)}, u32[]{:S(2)}) collective-permute-start(s32[128]{0:T(128)S(1)} %collective-permute-done.26), channel_id=1, source_target_pairs={{0,1},{1,2},{2,3},{3,4},{4,5},{5,6},{6,7},{7,8},{8,9},{9,10},{10,1... | collective-permute-start | bytes 1544 | tf_op jit(solution)/shard_map/ppermute | solution.py:14
  245.4 11.6 %collective-permute-start.15 = (bf16[128,1024]{1,0:T(8,128)(2,1)S(1)}, bf16[128,1024]{1,0:T(8,128)(2,1)S(1)}, u32[]{:S(2)}, u32[]{:S(2)}) collective-permute-start(bf16[128,1024]{1,0:T(8,128)(2,1)S(1)} %collective-permute-done.13), channel_id=1, source_target_pairs={{0,1},{1,2},{2,3},{3,4},{4,5},{5,6},{6,7},{7,8},{8,9},{9,10},{10,1... | collective-permute-start | bytes 786440 | tf_op jit(solution)/shard_map/ppermute | solution.py:14
  247.6 11.6 %collective-permute-start.31 = (f32[128]{0:T(128)S(1)}, f32[128]{0:T(128)S(1)}, u32[]{:S(2)}, u32[]{:S(2)}) collective-permute-start(f32[128]{0:T(128)S(1)} %broadcast_maximum_fusion), channel_id=1, source_target_pairs={{0,1},{1,2},{2,3},{3,4},{4,5},{5,6},{6,7},{7,8},{8,9},{9,10},{10,1... | collective-permute-start | bytes 1544 | tf_op jit(solution)/shard_map/ppermute | solution.py:14
  256.9 13.6 %collective-permute-start.17 = (bf16[128,1024]{1,0:T(8,128)(2,1)S(1)}, bf16[128,1024]{1,0:T(8,128)(2,1)S(1)}, u32[]{:S(2)}, u32[]{:S(2)}) collective-permute-start(bf16[128,1024]{1,0:T(8,128)(2,1)S(1)} %collective-permute-done.15), channel_id=1, source_target_pairs={{0,1},{1,2},{2,3},{3,4},{4,5},{5,6},{6,7},{7,8},{8,9},{9,10},{10,1... | collective-permute-start | bytes 786440 | tf_op jit(solution)/shard_map/ppermute | solution.py:14
  259.2 9.4 %collective-permute-start.33 = (f32[128]{0:T(128)S(1)}, f32[128]{0:T(128)S(1)}, u32[]{:S(2)}, u32[]{:S(2)}) collective-permute-start(f32[128]{0:T(128)S(1)} %max.885), channel_id=1, source_target_pairs={{0,1},{1,2},{2,3},{3,4},{4,5},{5,6},{6,7},{7,8},{8,9},{9,10},{10,1... | collective-permute-start | bytes 1544 | tf_op jit(solution)/shard_map/ppermute | solution.py:14
  270.5 17.5 %collective-permute-start.19 = (bf16[128,1024]{1,0:T(8,128)(2,1)S(1)}, bf16[128,1024]{1,0:T(8,128)(2,1)S(1)}, u32[]{:S(2)}, u32[]{:S(2)}) collective-permute-start(bf16[128,1024]{1,0:T(8,128)(2,1)S(1)} %collective-permute-done.17), channel_id=1, source_target_pairs={{0,1},{1,2},{2,3},{3,4},{4,5},{5,6},{6,7},{7,8},{8,9},{9,10},{10,1... | collective-permute-start | bytes 786440 | tf_op jit(solution)/shard_map/ppermute | solution.py:14
  288.0 17.5 %collective-permute-start.21 = (bf16[128,1024]{1,0:T(8,128)(2,1)S(1)}, bf16[128,1024]{1,0:T(8,128)(2,1)S(1)}, u32[]{:S(2)}, u32[]{:S(2)}) collective-permute-start(bf16[128,1024]{1,0:T(8,128)(2,1)S(1)} %collective-permute-done.19), channel_id=1, source_target_pairs={{0,1},{1,2},{2,3},{3,4},{4,5},{5,6},{6,7},{7,8},{8,9},{9,10},{10,1... | collective-permute-start | bytes 786440 | tf_op jit(solution)/shard_map/ppermute | solution.py:14
  305.5 17.5 %collective-permute-start.23 = (bf16[128,1024]{1,0:T(8,128)(2,1)S(1)}, bf16[128,1024]{1,0:T(8,128)(2,1)S(1)}, u32[]{:S(2)}, u32[]{:S(2)}) collective-permute-start(bf16[128,1024]{1,0:T(8,128)(2,1)S(1)} %collective-permute-done.21), channel_id=1, source_target_pairs={{0,1},{1,2},{2,3},{3,4},{4,5},{5,6},{6,7},{7,8},{8,9},{9,10},{10,1... | collective-permute-start | bytes 786440 | tf_op jit(solution)/shard_map/ppermute | solution.py:14
  312.3 8.7 %collective-permute-start.45 = (f32[128]{0:T(128)S(1)}, f32[128]{0:T(128)S(1)}, u32[]{:S(2)}, u32[]{:S(2)}) collective-permute-start(f32[128]{0:T(128)S(1)} %max.891), channel_id=1, source_target_pairs={{0,1},{1,2},{2,3},{3,4},{4,5},{5,6},{6,7},{7,8},{8,9},{9,10},{10,1... | collective-permute-start | bytes 1544 | tf_op jit(solution)/shard_map/ppermute | solution.py:14
  323.0 17.5 %collective-permute-start.25 = (bf16[128,1024]{1,0:T(8,128)(2,1)S(1)}, bf16[128,1024]{1,0:T(8,128)(2,1)S(1)}, u32[]{:S(2)}, u32[]{:S(2)}) collective-permute-start(bf16[128,1024]{1,0:T(8,128)(2,1)S(1)} %collective-permute-done.23), channel_id=1, source_target_pairs={{0,1},{1,2},{2,3},{3,4},{4,5},{5,6},{6,7},{7,8},{8,9},{9,10},{10,1... | collective-permute-start | bytes 786440 | tf_op jit(solution)/shard_map/ppermute | solution.py:14
  340.5 17.5 %collective-permute-start.27 = (bf16[128,1024]{1,0:T(8,128)(2,1)S(1)}, bf16[128,1024]{1,0:T(8,128)(2,1)S(1)}, u32[]{:S(2)}, u32[]{:S(2)}) collective-permute-start(bf16[128,1024]{1,0:T(8,128)(2,1)S(1)} %collective-permute-done.25), channel_id=1, source_target_pairs={{0,1},{1,2},{2,3},{3,4},{4,5},{5,6},{6,7},{7,8},{8,9},{9,10},{10,1... | collective-permute-start | bytes 786440 | tf_op jit(solution)/shard_map/ppermute | solution.py:14
  358.0 17.6 %collective-permute-start.29 = (bf16[128,1024]{1,0:T(8,128)(2,1)S(1)}, bf16[128,1024]{1,0:T(8,128)(2,1)S(1)}, u32[]{:S(2)}, u32[]{:S(2)}) collective-permute-start(bf16[128,1024]{1,0:T(8,128)(2,1)S(1)} %collective-permute-done.27), channel_id=1, source_target_pairs={{0,1},{1,2},{2,3},{3,4},{4,5},{5,6},{6,7},{7,8},{8,9},{9,10},{10,1... | collective-permute-start | bytes 786440 | tf_op jit(solution)/shard_map/ppermute | solution.py:14
  364.8 8.8 %collective-permute-start.57 = (f32[128]{0:T(128)S(1)}, f32[128]{0:T(128)S(1)}, u32[]{:S(2)}, u32[]{:S(2)}) collective-permute-start(f32[128]{0:T(128)S(1)} %max.897), channel_id=1, source_target_pairs={{0,1},{1,2},{2,3},{3,4},{4,5},{5,6},{6,7},{7,8},{8,9},{9,10},{10,1... | collective-permute-start | bytes 1544 | tf_op jit(solution)/shard_map/ppermute | solution.py:14
  383.0 14.5 %collective-permute-start.30 = (f32[128,1024]{1,0:T(8,128)S(1)}, f32[128,1024]{1,0:T(8,128)S(1)}, u32[]{:S(2)}, u32[]{:S(2)}) collective-permute-start(f32[128,1024]{1,0:T(8,128)S(1)} %convolution_add_fusion), channel_id=1, source_target_pairs={{0,1},{1,2},{2,3},{3,4},{4,5},{5,6},{6,7},{7,8},{8,9},{9,10},{10,1... | collective-permute-start | bytes 1572872 | tf_op jit(solution)/shard_map/ppermute | solution.py:14
  384.9 12.5 %collective-permute-start.61 = (f32[128]{0:T(128)S(1)}, f32[128]{0:T(128)S(1)}, u32[]{:S(2)}, u32[]{:S(2)}) collective-permute-start(f32[128]{0:T(128)S(1)} %get-tuple-element.151), channel_id=1, source_target_pairs={{0,1},{1,2},{2,3},{3,4},{4,5},{5,6},{6,7},{7,8},{8,9},{9,10},{10,1... | collective-permute-start | bytes 1544 | tf_op jit(solution)/shard_map/ppermute | solution.py:14
  397.8 14.5 %collective-permute-start.32 = (f32[128,1024]{1,0:T(8,128)S(1)}, f32[128,1024]{1,0:T(8,128)S(1)}, u32[]{:S(2)}, u32[]{:S(2)}) collective-permute-start(f32[128,1024]{1,0:T(8,128)S(1)} %multiply_add_fusion.14), channel_id=1, source_target_pairs={{0,1},{1,2},{2,3},{3,4},{4,5},{5,6},{6,7},{7,8},{8,9},{9,10},{10,1... | collective-permute-start | bytes 1572872 | tf_op jit(solution)/shard_map/ppermute | solution.py:14
  399.8 12.5 %collective-permute-start.62 = (f32[128]{0:T(128)S(1)}, f32[128]{0:T(128)S(1)}, u32[]{:S(2)}, u32[]{:S(2)}) collective-permute-start(f32[128]{0:T(128)S(1)} %get-tuple-element.118), channel_id=1, source_target_pairs={{0,1},{1,2},{2,3},{3,4},{4,5},{5,6},{6,7},{7,8},{8,9},{9,10},{10,1... | collective-permute-start | bytes 1544 | tf_op jit(solution)/shard_map/ppermute | solution.py:14
  412.7 15.5 %collective-permute-start.34 = (f32[128,1024]{1,0:T(8,128)S(1)}, f32[128,1024]{1,0:T(8,128)S(1)}, u32[]{:S(2)}, u32[]{:S(2)}) collective-permute-start(f32[128,1024]{1,0:T(8,128)S(1)} %multiply_add_fusion.13), channel_id=1, source_target_pairs={{0,1},{1,2},{2,3},{3,4},{4,5},{5,6},{6,7},{7,8},{8,9},{9,10},{10,1... | collective-permute-start | bytes 1572872 | tf_op jit(solution)/shard_map/ppermute | solution.py:14
  414.6 13.6 %collective-permute-start.63 = (f32[128]{0:T(128)S(1)}, f32[128]{0:T(128)S(1)}, u32[]{:S(2)}, u32[]{:S(2)}) collective-permute-start(f32[128]{0:T(128)S(1)} %get-tuple-element.116), channel_id=1, source_target_pairs={{0,1},{1,2},{2,3},{3,4},{4,5},{5,6},{6,7},{7,8},{8,9},{9,10},{10,1... | collective-permute-start | bytes 1544 | tf_op jit(solution)/shard_map/ppermute | solution.py:14
  428.5 17.0 %collective-permute-start.36 = (f32[128,1024]{1,0:T(8,128)S(1)}, f32[128,1024]{1,0:T(8,128)S(1)}, u32[]{:S(2)}, u32[]{:S(2)}) collective-permute-start(f32[128,1024]{1,0:T(8,128)S(1)} %multiply_add_fusion.12), channel_id=1, source_target_pairs={{0,1},{1,2},{2,3},{3,4},{4,5},{5,6},{6,7},{7,8},{8,9},{9,10},{10,1... | collective-permute-start | bytes 1572872 | tf_op jit(solution)/shard_map/ppermute | solution.py:14
  430.7 14.9 %collective-permute-start.64 = (f32[128]{0:T(128)S(1)}, f32[128]{0:T(128)S(1)}, u32[]{:S(2)}, u32[]{:S(2)}) collective-permute-start(f32[128]{0:T(128)S(1)} %get-tuple-element.114), channel_id=1, source_target_pairs={{0,1},{1,2},{2,3},{3,4},{4,5},{5,6},{6,7},{7,8},{8,9},{9,10},{10,1... | collective-permute-start | bytes 1544 | tf_op jit(solution)/shard_map/ppermute | solution.py:14
  445.9 17.9 %collective-permute-start.38 = (f32[128,1024]{1,0:T(8,128)S(1)}, f32[128,1024]{1,0:T(8,128)S(1)}, u32[]{:S(2)}, u32[]{:S(2)}) collective-permute-start(f32[128,1024]{1,0:T(8,128)S(1)} %multiply_add_fusion.11), channel_id=1, source_target_pairs={{0,1},{1,2},{2,3},{3,4},{4,5},{5,6},{6,7},{7,8},{8,9},{9,10},{10,1... | collective-permute-start | bytes 1572872 | tf_op jit(solution)/shard_map/ppermute | solution.py:14
  447.8 15.9 %collective-permute-start.65 = (f32[128]{0:T(128)S(1)}, f32[128]{0:T(128)S(1)}, u32[]{:S(2)}, u32[]{:S(2)}) collective-permute-start(f32[128]{0:T(128)S(1)} %get-tuple-element.112), channel_id=1, source_target_pairs={{0,1},{1,2},{2,3},{3,4},{4,5},{5,6},{6,7},{7,8},{8,9},{9,10},{10,1... | collective-permute-start | bytes 1544 | tf_op jit(solution)/shard_map/ppermute | solution.py:14
  464.1 19.0 %collective-permute-start.40 = (f32[128,1024]{1,0:T(8,128)S(1)}, f32[128,1024]{1,0:T(8,128)S(1)}, u32[]{:S(2)}, u32[]{:S(2)}) collective-permute-start(f32[128,1024]{1,0:T(8,128)S(1)} %multiply_add_fusion.10), channel_id=1, source_target_pairs={{0,1},{1,2},{2,3},{3,4},{4,5},{5,6},{6,7},{7,8},{8,9},{9,10},{10,1... | collective-permute-start | bytes 1572872 | tf_op jit(solution)/shard_map/ppermute | solution.py:14
  466.0 17.1 %collective-permute-start.66 = (f32[128]{0:T(128)S(1)}, f32[128]{0:T(128)S(1)}, u32[]{:S(2)}, u32[]{:S(2)}) collective-permute-start(f32[128]{0:T(128)S(1)} %get-tuple-element.110), channel_id=1, source_target_pairs={{0,1},{1,2},{2,3},{3,4},{4,5},{5,6},{6,7},{7,8},{8,9},{9,10},{10,1... | collective-permute-start | bytes 1544 | tf_op jit(solution)/shard_map/ppermute | solution.py:14
  483.5 20.0 %collective-permute-start.42 = (f32[128,1024]{1,0:T(8,128)S(1)}, f32[128,1024]{1,0:T(8,128)S(1)}, u32[]{:S(2)}, u32[]{:S(2)}) collective-permute-start(f32[128,1024]{1,0:T(8,128)S(1)} %multiply_add_fusion.9), channel_id=1, source_target_pairs={{0,1},{1,2},{2,3},{3,4},{4,5},{5,6},{6,7},{7,8},{8,9},{9,10},{10,1... | collective-permute-start | bytes 1572872 | tf_op jit(solution)/shard_map/ppermute | solution.py:14
  485.4 18.1 %collective-permute-start.67 = (f32[128]{0:T(128)S(1)}, f32[128]{0:T(128)S(1)}, u32[]{:S(2)}, u32[]{:S(2)}) collective-permute-start(f32[128]{0:T(128)S(1)} %get-tuple-element.108), channel_id=1, source_target_pairs={{0,1},{1,2},{2,3},{3,4},{4,5},{5,6},{6,7},{7,8},{8,9},{9,10},{10,1... | collective-permute-start | bytes 1544 | tf_op jit(solution)/shard_map/ppermute | solution.py:14
  503.8 19.1 %collective-permute-start.44 = (f32[128,1024]{1,0:T(8,128)S(1)}, f32[128,1024]{1,0:T(8,128)S(1)}, u32[]{:S(2)}, u32[]{:S(2)}) collective-permute-start(f32[128,1024]{1,0:T(8,128)S(1)} %multiply_add_fusion.8), channel_id=1, source_target_pairs={{0,1},{1,2},{2,3},{3,4},{4,5},{5,6},{6,7},{7,8},{8,9},{9,10},{10,1... | collective-permute-start | bytes 1572872 | tf_op jit(solution)/shard_map/ppermute | solution.py:14
  505.8 17.1 %collective-permute-start.68 = (f32[128]{0:T(128)S(1)}, f32[128]{0:T(128)S(1)}, u32[]{:S(2)}, u32[]{:S(2)}) collective-permute-start(f32[128]{0:T(128)S(1)} %get-tuple-element.106), channel_id=1, source_target_pairs={{0,1},{1,2},{2,3},{3,4},{4,5},{5,6},{6,7},{7,8},{8,9},{9,10},{10,1... | collective-permute-start | bytes 1544 | tf_op jit(solution)/shard_map/ppermute | solution.py:14
  523.3 18.2 %collective-permute-start.46 = (f32[128,1024]{1,0:T(8,128)S(1)}, f32[128,1024]{1,0:T(8,128)S(1)}, u32[]{:S(2)}, u32[]{:S(2)}) collective-permute-start(f32[128,1024]{1,0:T(8,128)S(1)} %multiply_add_fusion.7), channel_id=1, source_target_pairs={{0,1},{1,2},{2,3},{3,4},{4,5},{5,6},{6,7},{7,8},{8,9},{9,10},{10,1... | collective-permute-start | bytes 1572872 | tf_op jit(solution)/shard_map/ppermute | solution.py:14
  525.3 16.1 %collective-permute-start.69 = (f32[128]{0:T(128)S(1)}, f32[128]{0:T(128)S(1)}, u32[]{:S(2)}, u32[]{:S(2)}) collective-permute-start(f32[128]{0:T(128)S(1)} %get-tuple-element.104), channel_id=1, source_target_pairs={{0,1},{1,2},{2,3},{3,4},{4,5},{5,6},{6,7},{7,8},{8,9},{9,10},{10,1... | collective-permute-start | bytes 1544 | tf_op jit(solution)/shard_map/ppermute | solution.py:14
  541.8 17.2 %collective-permute-start.48 = (f32[128,1024]{1,0:T(8,128)S(1)}, f32[128,1024]{1,0:T(8,128)S(1)}, u32[]{:S(2)}, u32[]{:S(2)}) collective-permute-start(f32[128,1024]{1,0:T(8,128)S(1)} %multiply_add_fusion.6), channel_id=1, source_target_pairs={{0,1},{1,2},{2,3},{3,4},{4,5},{5,6},{6,7},{7,8},{8,9},{9,10},{10,1... | collective-permute-start | bytes 1572872 | tf_op jit(solution)/shard_map/ppermute | solution.py:14
  544.0 14.9 %collective-permute-start.70 = (f32[128]{0:T(128)S(1)}, f32[128]{0:T(128)S(1)}, u32[]{:S(2)}, u32[]{:S(2)}) collective-permute-start(f32[128]{0:T(128)S(1)} %get-tuple-element.102), channel_id=1, source_target_pairs={{0,1},{1,2},{2,3},{3,4},{4,5},{5,6},{6,7},{7,8},{8,9},{9,10},{10,1... | collective-permute-start | bytes 1544 | tf_op jit(solution)/shard_map/ppermute | solution.py:14
  559.3 16.2 %collective-permute-start.50 = (f32[128,1024]{1,0:T(8,128)S(1)}, f32[128,1024]{1,0:T(8,128)S(1)}, u32[]{:S(2)}, u32[]{:S(2)}) collective-permute-start(f32[128,1024]{1,0:T(8,128)S(1)} %multiply_add_fusion.5), channel_id=1, source_target_pairs={{0,1},{1,2},{2,3},{3,4},{4,5},{5,6},{6,7},{7,8},{8,9},{9,10},{10,1... | collective-permute-start | bytes 1572872 | tf_op jit(solution)/shard_map/ppermute | solution.py:14
  561.5 13.9 %collective-permute-start.71 = (f32[128]{0:T(128)S(1)}, f32[128]{0:T(128)S(1)}, u32[]{:S(2)}, u32[]{:S(2)}) collective-permute-start(f32[128]{0:T(128)S(1)} %get-tuple-element.100), channel_id=1, source_target_pairs={{0,1},{1,2},{2,3},{3,4},{4,5},{5,6},{6,7},{7,8},{8,9},{9,10},{10,1... | collective-permute-start | bytes 1544 | tf_op jit(solution)/shard_map/ppermute | solution.py:14
  575.8 15.2 %collective-permute-start.52 = (f32[128,1024]{1,0:T(8,128)S(1)}, f32[128,1024]{1,0:T(8,128)S(1)}, u32[]{:S(2)}, u32[]{:S(2)}) collective-permute-start(f32[128,1024]{1,0:T(8,128)S(1)} %multiply_add_fusion.4), channel_id=1, source_target_pairs={{0,1},{1,2},{2,3},{3,4},{4,5},{5,6},{6,7},{7,8},{8,9},{9,10},{10,1... | collective-permute-start | bytes 1572872 | tf_op jit(solution)/shard_map/ppermute | solution.py:14
  578.1 12.9 %collective-permute-start.72 = (f32[128]{0:T(128)S(1)}, f32[128]{0:T(128)S(1)}, u32[]{:S(2)}, u32[]{:S(2)}) collective-permute-start(f32[128]{0:T(128)S(1)} %get-tuple-element.98), channel_id=1, source_target_pairs={{0,1},{1,2},{2,3},{3,4},{4,5},{5,6},{6,7},{7,8},{8,9},{9,10},{10,1... | collective-permute-start | bytes 1544 | tf_op jit(solution)/shard_map/ppermute | solution.py:14
  591.4 14.5 %collective-permute-start.54 = (f32[128,1024]{1,0:T(8,128)S(1)}, f32[128,1024]{1,0:T(8,128)S(1)}, u32[]{:S(2)}, u32[]{:S(2)}) collective-permute-start(f32[128,1024]{1,0:T(8,128)S(1)} %multiply_add_fusion.3), channel_id=1, source_target_pairs={{0,1},{1,2},{2,3},{3,4},{4,5},{5,6},{6,7},{7,8},{8,9},{9,10},{10,1... | collective-permute-start | bytes 1572872 | tf_op jit(solution)/shard_map/ppermute | solution.py:14
  593.6 12.2 %collective-permute-start.73 = (f32[128]{0:T(128)S(1)}, f32[128]{0:T(128)S(1)}, u32[]{:S(2)}, u32[]{:S(2)}) collective-permute-start(f32[128]{0:T(128)S(1)} %get-tuple-element.96), channel_id=1, source_target_pairs={{0,1},{1,2},{2,3},{3,4},{4,5},{5,6},{6,7},{7,8},{8,9},{9,10},{10,1... | collective-permute-start | bytes 1544 | tf_op jit(solution)/shard_map/ppermute | solution.py:14
  606.2 14.5 %collective-permute-start.56 = (f32[128,1024]{1,0:T(8,128)S(1)}, f32[128,1024]{1,0:T(8,128)S(1)}, u32[]{:S(2)}, u32[]{:S(2)}) collective-permute-start(f32[128,1024]{1,0:T(8,128)S(1)} %multiply_add_fusion.2), channel_id=1, source_target_pairs={{0,1},{1,2},{2,3},{3,4},{4,5},{5,6},{6,7},{7,8},{8,9},{9,10},{10,1... | collective-permute-start | bytes 1572872 | tf_op jit(solution)/shard_map/ppermute | solution.py:14
  608.4 12.2 %collective-permute-start.74 = (f32[128]{0:T(128)S(1)}, f32[128]{0:T(128)S(1)}, u32[]{:S(2)}, u32[]{:S(2)}) collective-permute-start(f32[128]{0:T(128)S(1)} %get-tuple-element.94), channel_id=1, source_target_pairs={{0,1},{1,2},{2,3},{3,4},{4,5},{5,6},{6,7},{7,8},{8,9},{9,10},{10,1... | collective-permute-start | bytes 1544 | tf_op jit(solution)/shard_map/ppermute | solution.py:14
  621.0 14.5 %collective-permute-start.58 = (f32[128,1024]{1,0:T(8,128)S(1)}, f32[128,1024]{1,0:T(8,128)S(1)}, u32[]{:S(2)}, u32[]{:S(2)}) collective-permute-start(f32[128,1024]{1,0:T(8,128)S(1)} %multiply_add_fusion.1), channel_id=1, source_target_pairs={{0,1},{1,2},{2,3},{3,4},{4,5},{5,6},{6,7},{7,8},{8,9},{9,10},{10,1... | collective-permute-start | bytes 1572872 | tf_op jit(solution)/shard_map/ppermute | solution.py:14
  623.2 12.2 %collective-permute-start.75 = (f32[128]{0:T(128)S(1)}, f32[128]{0:T(128)S(1)}, u32[]{:S(2)}, u32[]{:S(2)}) collective-permute-start(f32[128]{0:T(128)S(1)} %get-tuple-element.92), channel_id=1, source_target_pairs={{0,1},{1,2},{2,3},{3,4},{4,5},{5,6},{6,7},{7,8},{8,9},{9,10},{10,1... | collective-permute-start | bytes 1544 | tf_op jit(solution)/shard_map/ppermute | solution.py:14
  635.8 14.5 %collective-permute-start.60 = (f32[128,1024]{1,0:T(8,128)S(1)}, f32[128,1024]{1,0:T(8,128)S(1)}, u32[]{:S(2)}, u32[]{:S(2)}) collective-permute-start(f32[128,1024]{1,0:T(8,128)S(1)} %multiply_add_fusion), channel_id=1, source_target_pairs={{0,1},{1,2},{2,3},{3,4},{4,5},{5,6},{6,7},{7,8},{8,9},{9,10},{10,1... | collective-permute-start | bytes 1572872 | tf_op jit(solution)/shard_map/ppermute | solution.py:14
  638.3 11.9 %collective-permute-start.76 = (f32[128]{0:T(128)S(1)}, f32[128]{0:T(128)S(1)}, u32[]{:S(2)}, u32[]{:S(2)}) collective-permute-start(f32[128]{0:T(128)S(1)} %get-tuple-element.90), channel_id=1, source_target_pairs={{0,1},{1,2},{2,3},{3,4},{4,5},{5,6},{6,7},{7,8},{8,9},{9,10},{10,1... | collective-permute-start | bytes 1544 | tf_op jit(solution)/shard_map/ppermute | solution.py:14
  (18 other events, 191.2 us)
where the time goes:
time: 655 us; the launch traced here: 651 us
  waiting for transfers between devices  448 us (68%)
  starting transfers between devices  174 us (27%)
  matrix products  16.1 us (2%)
  local copies, waits for them, and re-layouts  6.85 us (1%)
    ppermute x77, waiting for transfers between devices, shifted(): return lax.ppermute(value, axis, pairs)  430 us
    ppermute x77, starting transfers between devices, shifted(): return lax.ppermute(value, axis, pairs)  149 us
    all_to_all x1, starting transfers between devices, on_device(): lax.all_to_all(placed_bucket, 'src', split_axis=0, concat_axis=0, tiled=T...  15.4 us
  transfers between devices with their start and end apart: 80, of which 52 were waited for; matrix products, arithmetic and copies ran while one was open for 3% of the time, Pallas kernels for 0%

commit v1 on v0

v1 whole, which is shorter than its diff:
```python
import math

import jax
import jax.numpy as jnp
from jax import lax
from jax.sharding import PartitionSpec as P

lowest = -1e30


def shifted(value, axis, steps):
    count = lax.axis_size(axis)
    pairs = [(source, (source + steps) % count) for source in range(count)]
    return lax.ppermute(value, axis, pairs)


def allowed_mask(x_bucket, x_band, y_bucket, groups):
    near = jnp.abs(x_bucket[:, None] - y_bucket[None, :]) <= x_band[:, None]
    same = x_bucket[:, None] // groups == y_bucket[None, :] // groups
    return near & same


def on_device(source, target, src_bucket, tgt_bucket, band, route, bucket_group):
    row_count, feature_count = source.shape
    src_count = lax.axis_size("src")
    tgt_count = lax.axis_size("tgt")
    per_peer = row_count // src_count
    scaling = 2.0 / math.sqrt(feature_count)

    t_left = shifted((target, tgt_bucket), "tgt", 1)
    t_right = shifted((target, tgt_bucket), "tgt", -1)

    dest_slot = route // (row_count * tgt_count) * per_peer + route % per_peer
    placed = jnp.zeros_like(source).at[dest_slot].set(source)
    labels = jnp.stack([src_bucket, band], axis=1)
    placed_labels = jnp.zeros_like(labels).at[dest_slot].set(labels)
    sources = lax.all_to_all(placed, "src", split_axis=0, concat_axis=0, tiled=True)
    got_labels = lax.all_to_all(placed_labels, "src", split_axis=0, concat_axis=0, tiled=True)
    x_bucket, x_band = got_labels[:, 0], got_labels[:, 1]

    x_left = shifted((sources, x_bucket, x_band), "tgt", 1)
    x_right = shifted((sources, x_bucket, x_band), "tgt", -1)

    y_all = jnp.concatenate([t_left[0], target, t_right[0]], axis=0)
    y_bucket = jnp.concatenate([t_left[1], tgt_bucket, t_right[1]], axis=0)
    scores = lax.dot_general(
        sources, y_all, (((1,), (1,)), ((), ())), preferred_element_type=jnp.float32
    ) * scaling
    allowed = allowed_mask(x_bucket, x_band, y_bucket, bucket_group)
    masked = jnp.where(allowed, scores, lowest)
    row_top = jnp.max(masked, axis=1, keepdims=True)
    row_weights = jnp.where(allowed, jnp.exp(masked - row_top), 0.0)
    src_read = jnp.dot(
        row_weights.astype(jnp.bfloat16), y_all, preferred_element_type=jnp.float32
    ) / jnp.sum(row_weights, axis=1, keepdims=True)

    xs_all = jnp.concatenate([x_left[0], sources, x_right[0]], axis=0)
    xs_bucket = jnp.concatenate([x_left[1], x_bucket, x_right[1]], axis=0)
    xs_band = jnp.concatenate([x_left[2], x_band, x_right[2]], axis=0)
    col_scores = lax.dot_general(
        xs_all, target, (((1,), (1,)), ((), ())), preferred_element_type=jnp.float32
    ) * scaling
    col_allowed = allowed_mask(xs_bucket, xs_band, tgt_bucket, bucket_group)
    col_masked = jnp.where(col_allowed, col_scores, lowest)
    col_top = jnp.max(col_masked, axis=0, keepdims=True)
    col_weights = jnp.where(col_allowed, jnp.exp(col_masked - col_top), 0.0)
    tgt_read = lax.dot_general(
        col_weights.astype(jnp.bfloat16),
        xs_all,
        (((0,), (0,)), ((), ())),
        preferred_element_type=jnp.float32,
    ) / jnp.sum(col_weights, axis=0)[:, None]
    return (src_read, tgt_read)


def solution(mesh):
    placed = (
        P(("src", "tgt"), None),
        P(("src", "tgt"), None),
        P(("src", "tgt")),
        P(("src", "tgt")),
        P(("src", "tgt")),
        P(("src", "tgt")),
    )
    bucket_group = 128

    def body(*args):
        return on_device(*args, bucket_group)

    return jax.shard_map(
        body,
        mesh=mesh,
        in_specs=placed,
        out_specs=(P(("src", "tgt"), None), P(("src", "tgt"), None)),
        check_vma=False,
    )
```

time: 655 us -> 94.7 us (0.14)
  the two profiles are of different devices: /device:TPU:32 before, /device:TPU:30 now
where the time goes in v1:
time: 94.7 us; the launch traced here: 94.1 us
  starting transfers between devices  60 us (63%)
  waiting for transfers between devices  21.8 us (23%)
  local copies, waits for them, and re-layouts  6.85 us (7%)
  matrix products  3.39 us (4%)
  other arithmetic  1.2 us (1%)
    ppermute x10, starting transfers between devices, shifted(): return lax.ppermute(value, axis, pairs)  46 us
    all_to_all x1, starting transfers between devices, on_device(): lax.all_to_all(placed_labels, 'src', split_axis=0, concat_axis=0, tiled=T...  10.1 us
    ppermute x10, waiting for transfers between devices, shifted(): return lax.ppermute(value, axis, pairs)  9.9 us
    all_to_all x1, waiting for transfers between devices, on_device(): lax.all_to_all(placed_labels, 'src', split_axis=0, concat_axis=0, tiled=T...  9.86 us
    all_to_all x1, starting transfers between devices, on_device(): lax.all_to_all(placed, 'src', split_axis=0, concat_axis=0, tiled=True)  3.87 us
    unnamed x13, local copies, waits for them, and re-layouts  2.29 us
    all_to_all x1, waiting for transfers between devices, on_device(): lax.all_to_all(placed, 'src', split_axis=0, concat_axis=0, tiled=True)  2 us
  transfers between devices with their start and end apart: 12, of which 5 were waited for; matrix products, arithmetic and copies ran while one was open for 7% of the time, Pallas kernels for 0%

profile of v1, /device:TPU:30, one launch (start us, length us, event | category | flops | bytes accessed | tf_op | source)
XLA Modules:
  0.0 94.1 jit_solution(7965688405667352013)
XLA Ops:
  0.6 7.4 %collective-permute-start.2 = (bf16[128,1024]{1,0:T(8,128)(2,1)}, bf16[128,1024]{1,0:T(8,128)(2,1)S(1)}, u32[]{:S(2)}, u32[]{:S(2)}) collective-permute-start(bf16[128,1024]{1,0:T(8,128)(2,1)} %param.7), channel_id=1, source_target_pairs={{0,1},{1,2},{2,3},{3,4},{4,5},{5,6},{6,7},{7,8},{8,9},{9,10},{10,1... | collective-permute-start | bytes 786440 | tf_op jit(solution)/shard_map/ppermute | solution.py:14
  8.1 1.9 %collective-permute-start.3 = (bf16[128,1024]{1,0:T(8,128)(2,1)}, bf16[128,1024]{1,0:T(8,128)(2,1)S(1)}, u32[]{:S(2)}, u32[]{:S(2)}) collective-permute-start(bf16[128,1024]{1,0:T(8,128)(2,1)} %param.7), channel_id=1, source_target_pairs={{0,15},{1,0},{2,1},{3,2},{4,3},{5,4},{6,5},{7,6},{8,7},{9,8},{10,9... | collective-permute-start | bytes 786440 | tf_op jit(solution)/shard_map/ppermute | solution.py:14
  10.0 7.2 %collective-permute-start = (s32[128]{0:T(128)}, s32[128]{0:T(128)S(1)}, u32[]{:S(2)}, u32[]{:S(2)}) collective-permute-start(s32[128]{0:T(128)} %param.9), channel_id=1, source_target_pairs={{0,1},{1,2},{2,3},{3,4},{4,5},{5,6},{6,7},{7,8},{8,9},{9,10},{10,1... | collective-permute-start | bytes 1544 | tf_op jit(solution)/shard_map/ppermute | solution.py:14
  17.2 1.9 %collective-permute-start.1 = (s32[128]{0:T(128)}, s32[128]{0:T(128)S(1)}, u32[]{:S(2)}, u32[]{:S(2)}) collective-permute-start(s32[128]{0:T(128)} %param.9), channel_id=1, source_target_pairs={{0,15},{1,0},{2,1},{3,2},{4,3},{5,4},{6,5},{7,6},{8,7},{9,8},{10,9... | collective-permute-start | bytes 1544 | tf_op jit(solution)/shard_map/ppermute | solution.py:14
  19.2 0.7 compare_select_fusion
  19.8 0.0 copy-start.2
  19.9 0.0 copy-start.3
  19.9 0.6 copy-done.2
  20.5 0.0 copy-done.3
  20.5 0.1 copy.10
  20.6 0.9 scatter_custom_fusion
  21.5 0.9 copy.12
  22.4 10.1 %all-to-all-start = ((s32[32,4,2]{1,2,0:T(2,128)}), s32[32,4,2]{1,2,0:T(2,128)S(1)}, u32[]{:S(2)}, u32[]{:S(2)}) async-start(s32[32,4,2]{1,2,0:T(2,128)} %copy.12), calls=%async_computation | async-start | bytes 65536 | tf_op jit(solution)/shard_map/all_to_all | solution.py:38
  32.6 1.6 %scatter_custom_fusion.1 = bf16[128,1024]{1,0:T(8,128)(2,1)S(1)} fusion(s32[128]{0:T(128)S(1)} %compare_select_fusion, bf16[128,1024]{1,0:T(8,128)(2,1)} %param.6, bf16[]{:T(256)} %constant.81.clone.1), kind=kCustom, calls=%fused_computation.18 | custom fusion | bytes 262656 | tf_op jit(solution)/shard_map/scatter | solution.py:34
  34.2 0.8 all_to_all.19
  35.0 0.0 copy-start.1
  35.0 0.0 collective-permute-done
  35.0 0.6 copy-done.1
  35.7 0.0 collective-permute-done.1
  35.7 9.9 %all-to-all-done = s32[32,4,2]{1,2,0:T(2,128)S(1)} async-done(((s32[32,4,2]{1,2,0:T(2,128)}), s32[32,4,2]{1,2,0:T(2,128)S(1)}, u32[]{:S(2)}, u32[]{:S(2)}) %all-to-all-start) | async-done | bytes 1056 | tf_op jit(solution)/shard_map/all_to_all | solution.py:38
  45.6 3.9 %all-to-all-start.1 = ((bf16[32,4,1024]{2,1,0:T(4,128)(2,1)}), bf16[32,4,1024]{2,1,0:T(4,128)(2,1)S(1)}, u32[]{:S(2)}, u32[]{:S(2)}) async-start(bf16[32,4,1024]{2,1,0:T(4,128)(2,1)} %all_to_all.19), calls=%async_computation.1 | async-start | bytes 524288 | tf_op jit(solution)/shard_map/all_to_all | solution.py:37
  49.5 0.1 all_to_all.18
  49.6 1.9 %collective-permute-start.5 = (s32[128]{0:T(128)S(1)}, s32[128]{0:T(128)S(1)}, u32[]{:S(2)}, u32[]{:S(2)}) collective-permute-start(s32[128]{0:T(128)S(1)} %get-tuple-element.4), channel_id=1, source_target_pairs={{0,15},{1,0},{2,1},{3,2},{4,3},{5,4},{6,5},{7,6},{8,7},{9,8},{10,9... | collective-permute-start | bytes 1544 | tf_op jit(solution)/shard_map/ppermute | solution.py:14
  51.5 7.2 %collective-permute-start.4 = (s32[128]{0:T(128)S(1)}, s32[128]{0:T(128)S(1)}, u32[]{:S(2)}, u32[]{:S(2)}) collective-permute-start(s32[128]{0:T(128)S(1)} %get-tuple-element.4), channel_id=1, source_target_pairs={{0,1},{1,2},{2,3},{3,4},{4,5},{5,6},{6,7},{7,8},{8,9},{9,10},{10,1... | collective-permute-start | bytes 1544 | tf_op jit(solution)/shard_map/ppermute | solution.py:14
  58.8 1.9 %collective-permute-start.7 = (s32[128]{0:T(128)S(1)}, s32[128]{0:T(128)S(1)}, u32[]{:S(2)}, u32[]{:S(2)}) collective-permute-start(s32[128]{0:T(128)S(1)} %get-tuple-element.6), channel_id=1, source_target_pairs={{0,15},{1,0},{2,1},{3,2},{4,3},{5,4},{6,5},{7,6},{8,7},{9,8},{10,9... | collective-permute-start | bytes 1544 | tf_op jit(solution)/shard_map/ppermute | solution.py:14
  60.7 0.0 collective-permute-done.5
  60.7 7.2 %collective-permute-start.6 = (s32[128]{0:T(128)S(1)}, s32[128]{0:T(128)S(1)}, u32[]{:S(2)}, u32[]{:S(2)}) collective-permute-start(s32[128]{0:T(128)S(1)} %get-tuple-element.6), channel_id=1, source_target_pairs={{0,1},{1,2},{2,3},{3,4},{4,5},{5,6},{6,7},{7,8},{8,9},{9,10},{10,1... | collective-permute-start | bytes 1544 | tf_op jit(solution)/shard_map/ppermute | solution.py:14
  68.0 0.0 collective-permute-done.4
  68.0 0.0 collective-permute-done.7
  68.0 1.2 %collective-permute-done.6 = s32[128]{0:T(128)S(1)} collective-permute-done((s32[128]{0:T(128)S(1)}, s32[128]{0:T(128)S(1)}, u32[]{:S(2)}, u32[]{:S(2)}) %collective-permute-start.6) | collective-permute-done | bytes 544 | tf_op jit(solution)/shard_map/ppermute | solution.py:14
  69.2 0.0 copy-start
  69.2 0.0 collective-permute-done.2
  69.3 0.9 copy-done
  70.2 0.0 collective-permute-done.3
  70.2 2.0 %all-to-all-done.1 = bf16[32,4,1024]{2,1,0:T(4,128)(2,1)S(1)} async-done(((bf16[32,4,1024]{2,1,0:T(4,128)(2,1)}), bf16[32,4,1024]{2,1,0:T(4,128)(2,1)S(1)}, u32[]{:S(2)}, u32[]{:S(2)}) %all-to-all-start.1) | async-done | bytes 262176 | tf_op jit(solution)/shard_map/all_to_all | solution.py:37
  72.2 0.1 all_to_all.21
  72.3 7.2 %collective-permute-start.8 = (bf16[128,1024]{1,0:T(8,128)(2,1)S(1)}, bf16[128,1024]{1,0:T(8,128)(2,1)S(1)}, u32[]{:S(2)}, u32[]{:S(2)}) collective-permute-start(bf16[128,1024]{1,0:T(8,128)(2,1)S(1)} %all_to_all.21), channel_id=1, source_target_pairs={{0,1},{1,2},{2,3},{3,4},{4,5},{5,6},{6,7},{7,8},{8,9},{9,10},{10,1... | collective-permute-start | bytes 786440 | tf_op jit(solution)/shard_map/ppermute | solution.py:14
  79.6 1.9 %collective-permute-start.9 = (bf16[128,1024]{1,0:T(8,128)(2,1)S(1)}, bf16[128,1024]{1,0:T(8,128)(2,1)S(1)}, u32[]{:S(2)}, u32[]{:S(2)}) collective-permute-start(bf16[128,1024]{1,0:T(8,128)(2,1)S(1)} %all_to_all.21), channel_id=1, source_target_pairs={{0,15},{1,0},{2,1},{3,2},{4,3},{5,4},{6,5},{7,6},{8,7},{9,8},{10,9... | collective-permute-start | bytes 786440 | tf_op jit(solution)/shard_map/ppermute | solution.py:14
  81.5 0.5 fusion.28
  82.0 0.2 fusion.4
  82.2 1.2 %convolution_divide_fusion.1 = f32[128,1024]{1,0:T(8,128)} fusion(bf16[384,1024]{1,0:T(8,128)(2,1)S(1)} %constant_dynamic-update-slice_fusion.1, f32[128]{0:T(128)S(1)} %fusion.4, f32[128,384]{1,0:T(8,128)S(1)} %get-tuple-element.10, f32[128]{0:T(128)S(1)} %get-tuple-element.9, s32[384]{0:T(512)S(1)} %add_select_fusion.1, s32[128]{0:T(128)S(1)} %get-tuple-element.6, ...), kind=kOutput, calls=%fused_computation.3 | convolution fusion | flops 101187584 | bytes 1512960 | tf_op jit(solution)/shard_map/dot_general | solution.py:53
  83.4 1.3 %collective-permute-done.8 = bf16[128,1024]{1,0:T(8,128)(2,1)S(1)} collective-permute-done((bf16[128,1024]{1,0:T(8,128)(2,1)S(1)}, bf16[128,1024]{1,0:T(8,128)(2,1)S(1)}, u32[]{:S(2)}, u32[]{:S(2)}) %collective-permute-start.8) | collective-permute-done | bytes 262176 | tf_op jit(solution)/shard_map/ppermute | solution.py:14
  84.7 7.4 %collective-permute-done.9 = bf16[128,1024]{1,0:T(8,128)(2,1)S(1)} collective-permute-done((bf16[128,1024]{1,0:T(8,128)(2,1)S(1)}, bf16[128,1024]{1,0:T(8,128)(2,1)S(1)}, u32[]{:S(2)}, u32[]{:S(2)}) %collective-permute-start.9) | collective-permute-done | bytes 262176 | tf_op jit(solution)/shard_map/ppermute | solution.py:14
  92.1 0.4 fusion.29
  92.5 0.2 fusion.6
  92.7 1.3 %convolution_divide_fusion = f32[128,1024]{1,0:T(8,128)} fusion(bf16[384,1024]{1,0:T(8,128)(2,1)S(1)} %constant_dynamic-update-slice_fusion.4, f32[128]{0:T(128)S(1)} %fusion.6, f32[384,128]{1,0:T(8,128)S(1)} %get-tuple-element.12, f32[128]{0:T(128)S(1)} %get-tuple-element.11, s32[128]{0:T(128)S(1)} %get-tuple-element.7, s32[384]{0:T(512)S(1)} %pad_add_fusion.1, ...), kind=kOutput, calls=%fused_computation.2 | convolution fusion | flops 101187584 | bytes 1513984 | tf_op jit(solution)/shard_map/dot_general | solution.py:67
  (16 shorter events, 0.2 us)
Async XLA Ops:
  0.6 68.6 %collective-permute-start.2 = (bf16[128,1024]{1,0:T(8,128)(2,1)}, bf16[128,1024]{1,0:T(8,128)(2,1)S(1)}, u32[]{:S(2)}, u32[]{:S(2)}) collective-permute-start(bf16[128,1024]{1,0:T(8,128)(2,1)} %param.7), channel_id=1, source_target_pairs={{0,1},{1,2},{2,3},{3,4},{4,5},{5,6},{6,7},{7,8},{8,9},{9,10},{10,1... | collective-permute-start | bytes 786440 | tf_op jit(solution)/shard_map/ppermute | solution.py:14
  8.1 62.2 %collective-permute-start.3 = (bf16[128,1024]{1,0:T(8,128)(2,1)}, bf16[128,1024]{1,0:T(8,128)(2,1)S(1)}, u32[]{:S(2)}, u32[]{:S(2)}) collective-permute-start(bf16[128,1024]{1,0:T(8,128)(2,1)} %param.7), channel_id=1, source_target_pairs={{0,15},{1,0},{2,1},{3,2},{4,3},{5,4},{6,5},{7,6},{8,7},{9,8},{10,9... | collective-permute-start | bytes 786440 | tf_op jit(solution)/shard_map/ppermute | solution.py:14
  10.0 25.0 %collective-permute-start = (s32[128]{0:T(128)}, s32[128]{0:T(128)S(1)}, u32[]{:S(2)}, u32[]{:S(2)}) collective-permute-start(s32[128]{0:T(128)} %param.9), channel_id=1, source_target_pairs={{0,1},{1,2},{2,3},{3,4},{4,5},{5,6},{6,7},{7,8},{8,9},{9,10},{10,1... | collective-permute-start | bytes 1544 | tf_op jit(solution)/shard_map/ppermute | solution.py:14
  17.2 18.4 %collective-permute-start.1 = (s32[128]{0:T(128)}, s32[128]{0:T(128)S(1)}, u32[]{:S(2)}, u32[]{:S(2)}) collective-permute-start(s32[128]{0:T(128)} %param.9), channel_id=1, source_target_pairs={{0,15},{1,0},{2,1},{3,2},{4,3},{5,4},{6,5},{7,6},{8,7},{9,8},{10,9... | collective-permute-start | bytes 1544 | tf_op jit(solution)/shard_map/ppermute | solution.py:14
  19.8 0.7 copy-start.2
  19.9 0.7 copy-start.3
  22.4 23.1 %all-to-all-start = ((s32[32,4,2]{1,2,0:T(2,128)}), s32[32,4,2]{1,2,0:T(2,128)S(1)}, u32[]{:S(2)}, u32[]{:S(2)}) async-start(s32[32,4,2]{1,2,0:T(2,128)} %copy.12), calls=%async_computation | async-start | bytes 65536 | tf_op jit(solution)/shard_map/all_to_all | solution.py:38
  35.0 0.7 copy-start.1
  45.6 26.7 %all-to-all-start.1 = ((bf16[32,4,1024]{2,1,0:T(4,128)(2,1)}), bf16[32,4,1024]{2,1,0:T(4,128)(2,1)S(1)}, u32[]{:S(2)}, u32[]{:S(2)}) async-start(bf16[32,4,1024]{2,1,0:T(4,128)(2,1)} %all_to_all.19), calls=%async_computation.1 | async-start | bytes 524288 | tf_op jit(solution)/shard_map/all_to_all | solution.py:37
  49.6 11.1 %collective-permute-start.5 = (s32[128]{0:T(128)S(1)}, s32[128]{0:T(128)S(1)}, u32[]{:S(2)}, u32[]{:S(2)}) collective-permute-start(s32[128]{0:T(128)S(1)} %get-tuple-element.4), channel_id=1, source_target_pairs={{0,15},{1,0},{2,1},{3,2},{4,3},{5,4},{6,5},{7,6},{8,7},{9,8},{10,9... | collective-permute-start | bytes 1544 | tf_op jit(solution)/shard_map/ppermute | solution.py:14
  51.5 16.5 %collective-permute-start.4 = (s32[128]{0:T(128)S(1)}, s32[128]{0:T(128)S(1)}, u32[]{:S(2)}, u32[]{:S(2)}) collective-permute-start(s32[128]{0:T(128)S(1)} %get-tuple-element.4), channel_id=1, source_target_pairs={{0,1},{1,2},{2,3},{3,4},{4,5},{5,6},{6,7},{7,8},{8,9},{9,10},{10,1... | collective-permute-start | bytes 1544 | tf_op jit(solution)/shard_map/ppermute | solution.py:14
  58.8 9.2 %collective-permute-start.7 = (s32[128]{0:T(128)S(1)}, s32[128]{0:T(128)S(1)}, u32[]{:S(2)}, u32[]{:S(2)}) collective-permute-start(s32[128]{0:T(128)S(1)} %get-tuple-element.6), channel_id=1, source_target_pairs={{0,15},{1,0},{2,1},{3,2},{4,3},{5,4},{6,5},{7,6},{8,7},{9,8},{10,9... | collective-permute-start | bytes 1544 | tf_op jit(solution)/shard_map/ppermute | solution.py:14
  60.7 8.5 %collective-permute-start.6 = (s32[128]{0:T(128)S(1)}, s32[128]{0:T(128)S(1)}, u32[]{:S(2)}, u32[]{:S(2)}) collective-permute-start(s32[128]{0:T(128)S(1)} %get-tuple-element.6), channel_id=1, source_target_pairs={{0,1},{1,2},{2,3},{3,4},{4,5},{5,6},{6,7},{7,8},{8,9},{9,10},{10,1... | collective-permute-start | bytes 1544 | tf_op jit(solution)/shard_map/ppermute | solution.py:14
  69.2 0.9 %copy-start = (bf16[128,1024]{1,0:T(8,128)(2,1)S(1)}, bf16[128,1024]{1,0:T(8,128)(2,1)}, u32[]{:S(2)}) copy-start(bf16[128,1024]{1,0:T(8,128)(2,1)} %param.7) | copy-start | bytes 786436
  72.3 12.3 %collective-permute-start.8 = (bf16[128,1024]{1,0:T(8,128)(2,1)S(1)}, bf16[128,1024]{1,0:T(8,128)(2,1)S(1)}, u32[]{:S(2)}, u32[]{:S(2)}) collective-permute-start(bf16[128,1024]{1,0:T(8,128)(2,1)S(1)} %all_to_all.21), channel_id=1, source_target_pairs={{0,1},{1,2},{2,3},{3,4},{4,5},{5,6},{6,7},{7,8},{8,9},{9,10},{10,1... | collective-permute-start | bytes 786440 | tf_op jit(solution)/shard_map/ppermute | solution.py:14
  79.6 12.5 %collective-permute-start.9 = (bf16[128,1024]{1,0:T(8,128)(2,1)S(1)}, bf16[128,1024]{1,0:T(8,128)(2,1)S(1)}, u32[]{:S(2)}, u32[]{:S(2)}) collective-permute-start(bf16[128,1024]{1,0:T(8,128)(2,1)S(1)} %all_to_all.21), channel_id=1, source_target_pairs={{0,15},{1,0},{2,1},{3,2},{4,3},{5,4},{6,5},{7,6},{8,7},{9,8},{10,9... | collective-permute-start | bytes 786440 | tf_op jit(solution)/shard_map/ppermute | solution.py:14

commit v2 on v1

v2 whole, which is shorter than its diff:
```python
import functools
import math

import jax
import jax.numpy as jnp
from jax import lax
from jax.experimental import pallas as pl
from jax.experimental.pallas import tpu as pltpu
from jax.sharding import PartitionSpec as P

lowest = -1e30
MESH = pl.DeviceIdType.MESH
LABEL_LANES = 128
DIGIT = 64


def labelled(rows, columns):
    pad = jnp.zeros((rows.shape[0], LABEL_LANES - len(columns)), rows.dtype)
    labels = [c.astype(jnp.float32).astype(rows.dtype)[:, None] for c in columns]
    return jnp.concatenate([rows] + labels + [pad], axis=1)


def block_labels(block, features):
    slab = block[:, features:].astype(jnp.float32)
    as_cols = slab.astype(jnp.int32)
    as_rows = slab.T.astype(jnp.int32)
    return as_cols, as_rows


def kernel(groups, features, scaling, placed, target, src_out, tgt_out,
           xs, xl, xr, tl, tr, a2a_send, a2a_recv, nb_send, nb_recv, local_sem):
    g = lax.axis_index("src")
    t = lax.axis_index("tgt")
    n_src = lax.axis_size("src")
    n_tgt = lax.axis_size("tgt")
    span = placed.shape[0] // n_src
    left = lax.rem(t + n_tgt - 1, n_tgt)
    right = lax.rem(t + 1, n_tgt)

    barrier = pltpu.get_barrier_semaphore()

    def greet(d, carry):
        peer = lax.rem(g + d, n_src)
        pl.semaphore_signal(barrier, inc=1, device_id=(peer, t), device_id_type=MESH)
        return carry

    lax.fori_loop(1, n_src, greet, 0)
    pl.semaphore_signal(barrier, inc=1, device_id=(g, left), device_id_type=MESH)
    pl.semaphore_signal(barrier, inc=1, device_id=(g, right), device_id_type=MESH)
    pl.semaphore_wait(barrier, n_src + 1)

    t_to_right = pltpu.make_async_remote_copy(
        target, tl, nb_send.at[0], nb_recv.at[0], device_id=(g, right), device_id_type=MESH)
    t_to_left = pltpu.make_async_remote_copy(
        target, tr, nb_send.at[1], nb_recv.at[1], device_id=(g, left), device_id_type=MESH)
    t_to_right.start()
    t_to_left.start()

    def a2a_copy(peer):
        return pltpu.make_async_remote_copy(
            placed.at[pl.ds(peer * span, span)],
            xs.at[pl.ds(g * span, span)],
            a2a_send.at[peer],
            a2a_recv.at[g],
            device_id=(peer, t),
            device_id_type=MESH,
        )

    def a2a_start(d, carry):
        a2a_copy(lax.rem(g + d, n_src)).start()
        return carry

    lax.fori_loop(1, n_src, a2a_start, 0)
    own = pltpu.make_async_copy(
        placed.at[pl.ds(g * span, span)], xs.at[pl.ds(g * span, span)], local_sem.at[0])
    own.start()

    def a2a_wait(d, carry):
        peer = lax.rem(g + d, n_src)
        a2a_copy(peer).wait_send()
        sender = lax.rem(g + n_src - d, n_src)
        pltpu.make_async_remote_copy(
            placed.at[pl.ds(sender * span, span)],
            xs.at[pl.ds(sender * span, span)],
            a2a_send.at[sender],
            a2a_recv.at[sender],
            device_id=(sender, t),
            device_id_type=MESH,
        ).wait_recv()
        return carry

    lax.fori_loop(1, n_src, a2a_wait, 0)
    own.wait()

    x_to_right = pltpu.make_async_remote_copy(
        xs, xl, nb_send.at[2], nb_recv.at[2], device_id=(g, right), device_id_type=MESH)
    x_to_left = pltpu.make_async_remote_copy(
        xs, xr, nb_send.at[3], nb_recv.at[3], device_id=(g, left), device_id_type=MESH)
    x_to_right.start()
    x_to_left.start()

    t_to_right.wait()
    t_to_left.wait()

    x_main = xs[:, :features]
    x_cols, _ = block_labels(xs[...], features)
    x_bucket = x_cols[:, 0:1] * DIGIT + x_cols[:, 1:2]
    x_band = x_cols[:, 2:3]
    row_scores, row_masks = [], []
    for blk in (tl, target, tr):
        _, y_rows = block_labels(blk[...], features)
        y_bucket = y_rows[0:1, :] * DIGIT + y_rows[1:2, :]
        s = lax.dot_general(
            x_main, blk[:, :features], (((1,), (1,)), ((), ())),
            preferred_element_type=jnp.float32) * scaling
        ok = (jnp.abs(x_bucket - y_bucket) <= x_band) & (
            (x_bucket >> 7) == (y_bucket >> 7))
        row_scores.append(jnp.where(ok, s, lowest))
        row_masks.append(ok)
    top = functools.reduce(jnp.maximum, [jnp.max(s, axis=1, keepdims=True) for s in row_scores])
    total = jnp.zeros_like(top)
    read = jnp.zeros((x_main.shape[0], features), jnp.float32)
    for s, ok, blk in zip(row_scores, row_masks, (tl, target, tr)):
        w = jnp.where(ok, jnp.exp(s - top), 0.0)
        total = total + jnp.sum(w, axis=1, keepdims=True)
        read = read + jnp.dot(w.astype(jnp.bfloat16), blk[:, :features],
                              preferred_element_type=jnp.float32)
    src_out[...] = read / total

    x_to_right.wait()
    x_to_left.wait()

    y_main = target[:, :features]
    y_cols, _ = block_labels(target[...], features)
    y_bucket = y_cols[:, 0:1] * DIGIT + y_cols[:, 1:2]
    col_scores, col_masks = [], []
    for blk in (xl, xs, xr):
        _, s_rows = block_labels(blk[...], features)
        s_bucket = s_rows[0:1, :] * DIGIT + s_rows[1:2, :]
        s_band = s_rows[2:3, :]
        s = lax.dot_general(
            y_main, blk[:, :features], (((1,), (1,)), ((), ())),
            preferred_element_type=jnp.float32) * scaling
        ok = (jnp.abs(s_bucket - y_bucket) <= s_band) & (
            (s_bucket >> 7) == (y_bucket >> 7))
        col_scores.append(jnp.where(ok, s, lowest))
        col_masks.append(ok)
    top = functools.reduce(jnp.maximum, [jnp.max(s, axis=1, keepdims=True) for s in col_scores])
    total = jnp.zeros_like(top)
    read = jnp.zeros((y_main.shape[0], features), jnp.float32)
    for s, ok, blk in zip(col_scores, col_masks, (xl, xs, xr)):
        w = jnp.where(ok, jnp.exp(s - top), 0.0)
        total = total + jnp.sum(w, axis=1, keepdims=True)
        read = read + jnp.dot(w.astype(jnp.bfloat16), blk[:, :features],
                              preferred_element_type=jnp.float32)
    tgt_out[...] = read / total


def on_device(source, target, src_bucket, tgt_bucket, band, route):
    row_count, feature_count = source.shape
    src_count = lax.axis_size("src")
    tgt_count = lax.axis_size("tgt")
    per_peer = row_count // src_count
    scaling = 2.0 / math.sqrt(feature_count)
    groups = 128

    dest_slot = route // (row_count * tgt_count) * per_peer + route % per_peer
    src_lab = labelled(source, [src_bucket // DIGIT, src_bucket % DIGIT, band])
    placed = jnp.zeros_like(src_lab).at[dest_slot].set(src_lab)
    tgt_lab = labelled(target, [tgt_bucket // DIGIT, tgt_bucket % DIGIT])
    width = placed.shape[1]

    block = jax.ShapeDtypeStruct((row_count, feature_count), jnp.float32)
    vmem = pl.BlockSpec(memory_space=pltpu.VMEM)
    return pl.pallas_call(
        functools.partial(kernel, groups, feature_count, scaling),
        out_shape=(block, block),
        in_specs=[vmem, vmem],
        out_specs=(vmem, vmem),
        scratch_shapes=[pltpu.VMEM((row_count, width), jnp.bfloat16)] * 5
        + [
            pltpu.SemaphoreType.DMA((src_count,)),
            pltpu.SemaphoreType.DMA((src_count,)),
            pltpu.SemaphoreType.DMA((4,)),
            pltpu.SemaphoreType.DMA((4,)),
            pltpu.SemaphoreType.DMA((1,)),
        ],
        compiler_params=pltpu.CompilerParams(collective_id=0, has_side_effects=True),
    )(placed, tgt_lab)


def solution(mesh):
    placed = (
        P(("src", "tgt"), None),
        P(("src", "tgt"), None),
        P(("src", "tgt")),
        P(("src", "tgt")),
        P(("src", "tgt")),
        P(("src", "tgt")),
    )
    return jax.shard_map(
        on_device,
        mesh=mesh,
        in_specs=placed,
        out_specs=(P(("src", "tgt"), None), P(("src", "tgt"), None)),
        check_vma=False,
    )
```

time: 94.7 us -> 56 us (0.59)
  the two profiles are of different devices: /device:TPU:30 before, /device:TPU:1 now
where the time goes in v2:
time: 56 us; the launch traced here: 55.8 us
  Pallas kernels  46 us (82%)
  local copies, waits for them, and re-layouts  8.45 us (15%)
  other arithmetic  0.7 us (1%)
  between operations  0.69 us (1%)
    pallas_call x1, Pallas kernels, on_device(): pl.pallas_call(functools.partial(kernel, groups, feature_count, scaling),...  46 us
    unnamed x12, local copies, waits for them, and re-layouts  4.04 us
    concatenate x2, local copies, waits for them, and re-layouts, labelled(): return jnp.concatenate([rows] + labels + [pad], axis=1)  1.89 us
    scatter x1, local copies, waits for them, and re-layouts, on_device(): placed = jnp.zeros_like(src_lab).at[dest_slot].set(src_lab)  1.82 us

profile of v2, /device:TPU:1, one launch (start us, length us, event | category | flops | bytes accessed | tf_op | source)
XLA Modules:
  0.0 55.8 jit_solution(9280043668306379849)
XLA Ops:
  0.6 0.0 copy-start.2
  0.6 0.7 %convert_bitcast_fusion.1 = bf16[128,1]{0,1:T(2,128)(2,1)S(1)} fusion(s32[128]{0:T(128)} %param.10), kind=kLoop, calls=%fused_computation.28 | loop fusion | flops 256 | bytes 768 | tf_op jit(solution)/shard_map/broadcast_in_dim | solution.py:19
  1.3 0.0 copy-done.2
  1.3 0.0 copy-start.3
  1.3 0.6 %copy-done.3 = s32[128]{0:T(128)S(1)} copy-done((s32[128]{0:T(128)S(1)}, s32[128]{0:T(128)}, u32[]{:S(2)}) %copy-start.3) | copy-done | bytes 536
  2.0 0.0 copy-start.4
  2.0 0.6 %copy-done.4 = s32[128]{0:T(128)S(1)} copy-done((s32[128]{0:T(128)S(1)}, s32[128]{0:T(128)}, u32[]{:S(2)}) %copy-start.4) | copy-done | bytes 536
  2.6 0.1 copy.12
  2.8 0.1 copy.9
  2.9 0.1 copy.10
  3.1 0.1 copy.11
  3.2 0.1 copy.8
  3.3 1.1 %concatenate.6 = bf16[128,1152]{1,0:T(8,128)(2,1)S(1)} concatenate(bf16[128,1024]{1,0:T(8,128)(2,1)} %param.6, bf16[128,1]{1,0:T(8,128)(2,1)S(1)} %copy.8, bf16[128,1]{1,0:T(8,128)(2,1)S(1)} %copy.9, bf16[128,1]{1,0:T(8,128)(2,1)S(1)} %copy.10, bf16[128,125]{1,0:T(8,128)(2,1)S(1)} %broadcast_in_dim.32), dimensions={1} | concatenate | bytes 589824 | tf_op jit(solution)/shard_map/concatenate | solution.py:20
  4.4 0.0 copy-start.1
  4.4 1.8 %scatter_custom_fusion.placed = bf16[128,1152]{1,0:T(8,128)(2,1)} fusion(s32[128]{0:T(128)S(1)} %compare_select_fusion, bf16[128,1152]{1,0:T(8,128)(2,1)S(1)} %concatenate.6, bf16[]{:T(256)} %constant.58.clone.1), kind=kCustom, calls=%fused_computation.1 | custom fusion | bytes 294914 | tf_op jit(solution)/shard_map/scatter | solution.py:169
  6.3 0.0 copy-done.1
  6.3 0.8 %concatenate.7.target = bf16[128,1152]{1,0:T(8,128)(2,1)} concatenate(bf16[128,1024]{1,0:T(8,128)(2,1)S(1)} %copy-done.1, bf16[128,1]{1,0:T(8,128)(2,1)S(1)} %copy.11, bf16[128,1]{1,0:T(8,128)(2,1)S(1)} %copy.12, bf16[128,126]{1,0:T(8,128)(2,1)S(1)} %broadcast_in_dim.35), dimensions={1} | concatenate | bytes 589824 | tf_op jit(solution)/shard_map/concatenate | solution.py:20
  7.1 46.0 %shard_map.77 = (f32[128,1024]{1,0:T(8,128)}, f32[128,1024]{1,0:T(8,128)}) custom-call(bf16[128,1152]{1,0:T(8,128)(2,1)} %scatter_custom_fusion.placed, bf16[128,1152]{1,0:T(8,128)(2,1)} %concatenate.7.target), custom_call_target="tpu_custom_call" | custom-call | tf_op jit(solution)/shard_map/pallas_call | solution.py:175
  53.1 0.0 copy-start
  53.1 1.9 %copy.15 = f32[128,1024]{1,0:T(8,128)} copy(f32[128,1024]{1,0:T(8,128)} %get-tuple-element.8) | data formatting | bytes 1048576
  55.0 0.0 copy-done
  55.0 0.8 %copy.16 = f32[128,1024]{1,0:T(8,128)} copy(f32[128,1024]{1,0:T(8,128)S(1)} %copy-done) | data formatting | bytes 1048576
  (5 shorter events, 0.1 us)
Async XLA Ops:
  0.6 0.7 %copy-start.2 = (s32[128]{0:T(128)S(1)}, s32[128]{0:T(128)}, u32[]{:S(2)}) copy-start(s32[128]{0:T(128)} %param.11) | copy-start | bytes 1540
  1.3 0.7 %copy-start.3 = (s32[128]{0:T(128)S(1)}, s32[128]{0:T(128)}, u32[]{:S(2)}) copy-start(s32[128]{0:T(128)} %param.8) | copy-start | bytes 1540
  2.0 0.7 %copy-start.4 = (s32[128]{0:T(128)S(1)}, s32[128]{0:T(128)}, u32[]{:S(2)}) copy-start(s32[128]{0:T(128)} %param.9) | copy-start | bytes 1540
  4.4 1.8 %copy-start.1 = (bf16[128,1024]{1,0:T(8,128)(2,1)S(1)}, bf16[128,1024]{1,0:T(8,128)(2,1)}, u32[]{:S(2)}) copy-start(bf16[128,1024]{1,0:T(8,128)(2,1)} %param.7) | copy-start | bytes 786436
  53.1 2.0 %copy-start = (f32[128,1024]{1,0:T(8,128)S(1)}, f32[128,1024]{1,0:T(8,128)}, u32[]{:S(2)}) copy-start(f32[128,1024]{1,0:T(8,128)} %get-tuple-element.9) | copy-start | bytes 1572868

commit v3 on v1

v3 whole, which is shorter than its diff:
```python
import functools
import math

import jax
import jax.numpy as jnp
from jax import lax
from jax.experimental import pallas as pl
from jax.experimental.pallas import tpu as pltpu
from jax.sharding import PartitionSpec as P

lowest = -1e30
MESH = pl.DeviceIdType.MESH
LABEL_LANES = 128
DIGIT = 64
SRC_HI, SRC_LO, SRC_BAND, DEST, TGT_HI, TGT_LO = range(6)


def softmax_read(main, main_bucket, band_col, others, features, scaling, band_of_rows):
    scores, masks = [], []
    for blk, bucket_row, band_row in others:
        s = lax.dot_general(
            main, blk[:, :features], (((1,), (1,)), ((), ())),
            preferred_element_type=jnp.float32) * scaling
        band = band_col if band_of_rows else band_row
        ok = (jnp.abs(main_bucket - bucket_row) <= band) & (
            (main_bucket >> 7) == (bucket_row >> 7))
        scores.append(jnp.where(ok, s, lowest))
        masks.append(ok)
    top = functools.reduce(jnp.maximum, [jnp.max(s, axis=1, keepdims=True) for s in scores])
    total = jnp.zeros_like(top)
    read = jnp.zeros((main.shape[0], features), jnp.float32)
    for s, ok, (blk, _, _) in zip(scores, masks, others):
        w = jnp.where(ok, jnp.exp(s - top), 0.0)
        total = total + jnp.sum(w, axis=1, keepdims=True)
        read = read + jnp.dot(w.astype(jnp.bfloat16), blk[:, :features],
                              preferred_element_type=jnp.float32)
    return read / total


def label_rows(blk, features, hi, lo, band=None):
    slab = blk[:, features:].astype(jnp.float32).T.astype(jnp.int32)
    bucket = slab[hi:hi + 1, :] * DIGIT + slab[lo:lo + 1, :]
    return bucket, (slab[band:band + 1, :] if band is not None else None)


def kernel(features, scaling, source, target, lab, src_out, tgt_out,
           xsend, tsend, xs, xl, xr, tl, tr,
           a2a_send, a2a_recv, fw_send, fw_recv, nb_send, nb_recv, local_sem):
    g = lax.axis_index("src")
    t = lax.axis_index("tgt")
    n_src = lax.axis_size("src")
    n_tgt = lax.axis_size("tgt")
    rows = source.shape[0]
    span = rows // n_src
    n_z = n_src // 2
    z = g // 2
    core = g % 2
    partner = z * 2 + 1 - core
    left = lax.rem(t + n_tgt - 1, n_tgt)
    right = lax.rem(t + 1, n_tgt)

    def far_peer(j):
        kz = j // 2 + 1
        offset = ((kz + 1) // 2) * (2 * (kz % 2) - 1)
        return ((z + offset + n_z) % n_z) * 2 + j % 2

    barrier = pltpu.get_barrier_semaphore()
    pl.semaphore_signal(barrier, inc=1, device_id=(partner, t), device_id_type=MESH)

    def greet(j, carry):
        pl.semaphore_signal(barrier, inc=1, device_id=(far_peer(j), t), device_id_type=MESH)
        return carry

    lax.fori_loop(0, n_src - 2, greet, 0)
    pl.semaphore_signal(barrier, inc=1, device_id=(g, left), device_id_type=MESH)
    pl.semaphore_signal(barrier, inc=1, device_id=(g, right), device_id_type=MESH)

    table = lab[...]
    labels = table.T.astype(jnp.bfloat16)
    dest = table[DEST:DEST + 1, :].astype(jnp.int32)
    onehot = (lax.broadcasted_iota(jnp.int32, (rows, rows), 0) == dest).astype(jnp.bfloat16)
    xsend[:, :features] = jnp.dot(
        onehot, source[...], preferred_element_type=jnp.float32).astype(jnp.bfloat16)
    xsend[:, features:] = jnp.dot(
        onehot, labels, preferred_element_type=jnp.float32).astype(jnp.bfloat16)
    tsend[:, :features] = target[...]
    tsend[:, features:] = labels

    pl.semaphore_wait(barrier, n_src + 1)

    t_to_right = pltpu.make_async_remote_copy(
        tsend, tl, nb_send.at[0], nb_recv.at[0], device_id=(g, right), device_id_type=MESH)
    t_to_left = pltpu.make_async_remote_copy(
        tsend, tr, nb_send.at[1], nb_recv.at[1], device_id=(g, left), device_id_type=MESH)
    t_to_right.start()
    t_to_left.start()

    def a2a_copy(peer, sender):
        return pltpu.make_async_remote_copy(
            xsend.at[pl.ds(peer * span, span)],
            xs.at[pl.ds(sender * span, span)],
            a2a_send.at[peer],
            a2a_recv.at[sender],
            device_id=(peer, t),
            device_id_type=MESH,
        )

    own = pltpu.make_async_copy(
        xsend.at[pl.ds(g * span, span)], xs.at[pl.ds(g * span, span)], local_sem.at[0])
    own.start()
    a2a_copy(partner, g).start()

    def a2a_start(j, carry):
        a2a_copy(far_peer(j), g).start()
        return carry

    lax.fori_loop(0, n_src - 2, a2a_start, 0)

    def forward(sender):
        rows_of = pl.ds(sender * span, span)
        return (
            pltpu.make_async_remote_copy(
                xs.at[rows_of], xl.at[rows_of], fw_send.at[sender], fw_recv.at[sender],
                device_id=(g, right), device_id_type=MESH),
            pltpu.make_async_remote_copy(
                xs.at[rows_of], xr.at[rows_of], fw_send.at[n_src + sender],
                fw_recv.at[n_src + sender], device_id=(g, left), device_id_type=MESH),
        )

    def arrive_and_forward(sender):
        rows_of = pl.ds(sender * span, span)
        pltpu.make_async_remote_copy(
            xsend.at[rows_of], xs.at[rows_of], a2a_send.at[sender], a2a_recv.at[sender],
            device_id=(sender, t), device_id_type=MESH).wait_recv()
        for c in forward(sender):
            c.start()

    own.wait()
    for c in forward(g):
        c.start()
    arrive_and_forward(partner)

    def a2a_arrive(j, carry):
        arrive_and_forward(far_peer(j))
        return carry

    lax.fori_loop(0, n_src - 2, a2a_arrive, 0)

    t_to_right.wait()
    t_to_left.wait()

    x_cols = xs[:, features:].astype(jnp.float32).astype(jnp.int32)
    x_bucket = x_cols[:, SRC_HI:SRC_HI + 1] * DIGIT + x_cols[:, SRC_LO:SRC_LO + 1]
    x_band = x_cols[:, SRC_BAND:SRC_BAND + 1]
    tgt_blocks = []
    for blk in (tl, tsend, tr):
        bucket_row, _ = label_rows(blk[...], features, TGT_HI, TGT_LO)
        tgt_blocks.append((blk, bucket_row, None))
    src_out[...] = softmax_read(
        xs[:, :features], x_bucket, x_band, tgt_blocks, features, scaling, True)

    a2a_copy(partner, g).wait_send()

    def a2a_sent(j, carry):
        a2a_copy(far_peer(j), g).wait_send()
        return carry

    lax.fori_loop(0, n_src - 2, a2a_sent, 0)

    def fw_done(s, carry):
        for c in forward(s):
            c.wait_send()
            c.wait_recv()
        return carry

    lax.fori_loop(0, n_src, fw_done, 0)

    y_cols = tsend[:, features:].astype(jnp.float32).astype(jnp.int32)
    y_bucket = y_cols[:, TGT_HI:TGT_HI + 1] * DIGIT + y_cols[:, TGT_LO:TGT_LO + 1]
    src_blocks = []
    for blk in (xl, xs, xr):
        bucket_row, band_row = label_rows(blk[...], features, SRC_HI, SRC_LO, SRC_BAND)
        src_blocks.append((blk, bucket_row, band_row))
    tgt_out[...] = softmax_read(
        tsend[:, :features], y_bucket, None, src_blocks, features, scaling, False)


def on_device(source, target, src_bucket, tgt_bucket, band, route):
    row_count, feature_count = source.shape
    src_count = lax.axis_size("src")
    tgt_count = lax.axis_size("tgt")
    per_peer = row_count // src_count
    scaling = 2.0 / math.sqrt(feature_count)

    dest_slot = route // (row_count * tgt_count) * per_peer + route % per_peer
    table = jnp.stack(
        [src_bucket // DIGIT, src_bucket % DIGIT, band, dest_slot,
         tgt_bucket // DIGIT, tgt_bucket % DIGIT]).astype(jnp.float32)
    table = jnp.pad(table, ((0, LABEL_LANES - table.shape[0]), (0, 0)))
    width = feature_count + LABEL_LANES

    block = jax.ShapeDtypeStruct((row_count, feature_count), jnp.float32)
    vmem = pl.BlockSpec(memory_space=pltpu.VMEM)
    return pl.pallas_call(
        functools.partial(kernel, feature_count, scaling),
        out_shape=(block, block),
        in_specs=[vmem, vmem, vmem],
        out_specs=(vmem, vmem),
        scratch_shapes=[pltpu.VMEM((row_count, width), jnp.bfloat16)] * 7
        + [
            pltpu.SemaphoreType.DMA((src_count,)),
            pltpu.SemaphoreType.DMA((src_count,)),
            pltpu.SemaphoreType.DMA((2 * src_count,)),
            pltpu.SemaphoreType.DMA((2 * src_count,)),
            pltpu.SemaphoreType.DMA((2,)),
            pltpu.SemaphoreType.DMA((2,)),
            pltpu.SemaphoreType.DMA((1,)),
        ],
        compiler_params=pltpu.CompilerParams(collective_id=0, has_side_effects=True),
    )(source, target, table)


def solution(mesh):
    placed = (
        P(("src", "tgt"), None),
        P(("src", "tgt"), None),
        P(("src", "tgt")),
        P(("src", "tgt")),
        P(("src", "tgt")),
        P(("src", "tgt")),
    )
    return jax.shard_map(
        on_device,
        mesh=mesh,
        in_specs=placed,
        out_specs=(P(("src", "tgt"), None), P(("src", "tgt"), None)),
        check_vma=False,
    )
```

time: 94.7 us -> 49.3 us (0.52)
  the two profiles are of different devices: /device:TPU:30 before, /device:TPU:1 now
where the time goes in v3:
time: 49.3 us; the launch traced here: 48.5 us
  Pallas kernels  42.5 us (86%)
  local copies, waits for them, and re-layouts  5.36 us (11%)
  between operations  0.67 us (1%)
    pallas_call x1, Pallas kernels, on_device(): pl.pallas_call(functools.partial(kernel, feature_count, scaling), out_sha...  42.5 us
    unnamed x12, local copies, waits for them, and re-layouts  4.7 us

profile of v3, /device:TPU:1, one launch (start us, length us, event | category | flops | bytes accessed | tf_op | source)
XLA Modules:
  0.0 48.5 jit_solution(17361625857831023115)
XLA Ops:
  0.6 0.0 copy-start.4
  0.6 0.6 %copy-done.4 = s32[128]{0:T(128)S(1)} copy-done((s32[128]{0:T(128)S(1)}, s32[128]{0:T(128)}, u32[]{:S(2)}) %copy-start.4) | copy-done | bytes 536
  1.3 0.0 copy-start.2
  1.3 0.0 copy-start.3
  1.3 0.6 %copy-done.2 = s32[128]{0:T(128)S(1)} copy-done((s32[128]{0:T(128)S(1)}, s32[128]{0:T(128)}, u32[]{:S(2)}) %copy-start.2) | copy-done | bytes 536
  1.9 0.0 copy-done.3
  2.0 0.0 copy-start.1
  2.0 0.6 %copy-done.1 = s32[128]{0:T(128)S(1)} copy-done((s32[128]{0:T(128)S(1)}, s32[128]{0:T(128)}, u32[]{:S(2)}) %copy-start.1) | copy-done | bytes 536
  2.7 0.6 %pad.4.lab = f32[128,128]{1,0:T(8,128)} pad(f32[6,128]{1,0:T(8,128)S(1)} %convert_element_type.5, f32[]{:T(128)} %constant.65.clone.1), padding=0_122x0_0 | pad | bytes 68612 | tf_op jit(solution)/shard_map/jit(_pad)/pad | solution.py:199
  3.3 42.5 %shard_map.77 = (f32[128,1024]{1,0:T(8,128)}, f32[128,1024]{1,0:T(8,128)}) custom-call(bf16[128,1024]{1,0:T(8,128)(2,1)} %source.1, bf16[128,1024]{1,0:T(8,128)(2,1)} %target.1, f32[128,128]{1,0:T(8,128)} %pad.4.lab), custom_call_target="tpu_custom_call" | custom-call | tf_op jit(solution)/shard_map/pallas_call | solution.py:204
  45.8 0.0 copy-start
  45.8 1.9 %copy.10 = f32[128,1024]{1,0:T(8,128)} copy(f32[128,1024]{1,0:T(8,128)} %get-tuple-element.10) | data formatting | bytes 1048576
  47.7 0.0 copy-done
  47.7 0.8 %copy.11 = f32[128,1024]{1,0:T(8,128)} copy(f32[128,1024]{1,0:T(8,128)S(1)} %copy-done) | data formatting | bytes 1048576
  (4 shorter events, 0.1 us)
Async XLA Ops:
  0.6 0.7 %copy-start.4 = (s32[128]{0:T(128)S(1)}, s32[128]{0:T(128)}, u32[]{:S(2)}) copy-start(s32[128]{0:T(128)} %param.11) | copy-start | bytes 1540
  1.3 0.7 %copy-start.2 = (s32[128]{0:T(128)S(1)}, s32[128]{0:T(128)}, u32[]{:S(2)}) copy-start(s32[128]{0:T(128)} %param.8) | copy-start | bytes 1540
  1.3 0.7 %copy-start.3 = (s32[128]{0:T(128)S(1)}, s32[128]{0:T(128)}, u32[]{:S(2)}) copy-start(s32[128]{0:T(128)} %param.9) | copy-start | bytes 1540
  2.0 0.7 %copy-start.1 = (s32[128]{0:T(128)S(1)}, s32[128]{0:T(128)}, u32[]{:S(2)}) copy-start(s32[128]{0:T(128)} %param.10) | copy-start | bytes 1540
  45.8 2.0 %copy-start = (f32[128,1024]{1,0:T(8,128)S(1)}, f32[128,1024]{1,0:T(8,128)}, u32[]{:S(2)}) copy-start(f32[128,1024]{1,0:T(8,128)} %get-tuple-element.11) | copy-start | bytes 1572868

commit v4 on v3

--- a/solution.py
+++ b/solution.py
@@ -34,7 +34,7 @@
         total = total + jnp.sum(w, axis=1, keepdims=True)
         read = read + jnp.dot(w.astype(jnp.bfloat16), blk[:, :features],
                               preferred_element_type=jnp.float32)
-    return read / total
+    return read, total
 
 
 def label_rows(blk, features, hi, lo, band=None):
@@ -43,8 +43,8 @@
     return bucket, (slab[band:band + 1, :] if band is not None else None)
 
 
-def kernel(features, scaling, source, target, lab, src_out, tgt_out,
-           xsend, tsend, xs, xl, xr, tl, tr,
+def kernel(features, scaling, source_hbm, target_hbm, lab_hbm, src_out, tgt_out, src_total, tgt_total,
+           source, target, lab, xsend, tsend, xs, xl, xr, tl, tr,
            a2a_send, a2a_recv, fw_send, fw_recv, nb_send, nb_recv, local_sem):
     g = lax.axis_index("src")
     t = lax.axis_index("tgt")
@@ -64,6 +64,13 @@
         offset = ((kz + 1) // 2) * (2 * (kz % 2) - 1)
         return ((z + offset + n_z) % n_z) * 2 + j % 2
 
+    loads = [
+        pltpu.make_async_copy(hbm, vmem, local_sem.at[1 + i])
+        for i, (hbm, vmem) in enumerate(((source_hbm, source), (target_hbm, target), (lab_hbm, lab)))
+    ]
+    for c in loads:
+        c.start()
+
     barrier = pltpu.get_barrier_semaphore()
     pl.semaphore_signal(barrier, inc=1, device_id=(partner, t), device_id_type=MESH)
 
@@ -75,16 +82,28 @@
     pl.semaphore_signal(barrier, inc=1, device_id=(g, left), device_id_type=MESH)
     pl.semaphore_signal(barrier, inc=1, device_id=(g, right), device_id_type=MESH)
 
+    for c in loads:
+        c.wait()
+
     table = lab[...]
-    labels = table.T.astype(jnp.bfloat16)
-    dest = table[DEST:DEST + 1, :].astype(jnp.int32)
-    onehot = (lax.broadcasted_iota(jnp.int32, (rows, rows), 0) == dest).astype(jnp.bfloat16)
+    slot = lax.broadcasted_iota(jnp.int32, (rows, rows), 0)
+    lane = lax.broadcasted_iota(jnp.int32, (rows, LABEL_LANES), 1)
+    onehot = (slot == table[DEST:DEST + 1, :].astype(jnp.int32)).astype(jnp.float32)
+    ident = (slot == lax.broadcasted_iota(jnp.int32, (rows, rows), 1)).astype(jnp.float32)
+
+    def label_slab(select, kinds):
+        slab = jnp.zeros((rows, LABEL_LANES), jnp.float32)
+        for k in kinds:
+            column = jnp.sum(select * table[k:k + 1, :], axis=1, keepdims=True)
+            slab = jnp.where(lane == k, column, slab)
+        return slab.astype(jnp.bfloat16)
+
     xsend[:, :features] = jnp.dot(
-        onehot, source[...], preferred_element_type=jnp.float32).astype(jnp.bfloat16)
-    xsend[:, features:] = jnp.dot(
-        onehot, labels, preferred_element_type=jnp.float32).astype(jnp.bfloat16)
+        onehot.astype(jnp.bfloat16), source[...],
+        preferred_element_type=jnp.float32).astype(jnp.bfloat16)
+    xsend[:, features:] = label_slab(onehot, (SRC_HI, SRC_LO, SRC_BAND))
     tsend[:, :features] = target[...]
-    tsend[:, features:] = labels
+    tsend[:, features:] = label_slab(ident, (TGT_HI, TGT_LO))
 
     pl.semaphore_wait(barrier, n_src + 1)
 
@@ -156,7 +175,7 @@
     for blk in (tl, tsend, tr):
         bucket_row, _ = label_rows(blk[...], features, TGT_HI, TGT_LO)
         tgt_blocks.append((blk, bucket_row, None))
-    src_out[...] = softmax_read(
+    src_out[...], src_total[...] = softmax_read(
         xs[:, :features], x_bucket, x_band, tgt_blocks, features, scaling, True)
 
     a2a_copy(partner, g).wait_send()
@@ -181,7 +200,7 @@
     for blk in (xl, xs, xr):
         bucket_row, band_row = label_rows(blk[...], features, SRC_HI, SRC_LO, SRC_BAND)
         src_blocks.append((blk, bucket_row, band_row))
-    tgt_out[...] = softmax_read(
+    tgt_out[...], tgt_total[...] = softmax_read(
         tsend[:, :features], y_bucket, None, src_blocks, features, scaling, False)
 
 
@@ -196,17 +215,24 @@
     table = jnp.stack(
         [src_bucket // DIGIT, src_bucket % DIGIT, band, dest_slot,
          tgt_bucket // DIGIT, tgt_bucket % DIGIT]).astype(jnp.float32)
-    table = jnp.pad(table, ((0, LABEL_LANES - table.shape[0]), (0, 0)))
+    table = jnp.pad(table, ((0, 8 - table.shape[0]), (0, 0)))
     width = feature_count + LABEL_LANES
 
     block = jax.ShapeDtypeStruct((row_count, feature_count), jnp.float32)
+    totals = jax.ShapeDtypeStruct((row_count, 1), jnp.float32)
     vmem = pl.BlockSpec(memory_space=pltpu.VMEM)
-    return pl.pallas_call(
+    hbm = pl.BlockSpec(memory_space=pl.ANY)
+    src_read, tgt_read, src_total, tgt_total = pl.pallas_call(
         functools.partial(kernel, feature_count, scaling),
-        out_shape=(block, block),
-        in_specs=[vmem, vmem, vmem],
-        out_specs=(vmem, vmem),
-        scratch_shapes=[pltpu.VMEM((row_count, width), jnp.bfloat16)] * 7
+        out_shape=(block, block, totals, totals),
+        in_specs=[hbm, hbm, hbm],
+        out_specs=(vmem, vmem, vmem, vmem),
+        scratch_shapes=[
+            pltpu.VMEM((row_count, feature_count), jnp.bfloat16),
+            pltpu.VMEM((row_count, feature_count), jnp.bfloat16),
+            pltpu.VMEM(table.shape, jnp.float32),
+        ]
+        + [pltpu.VMEM((row_count, width), jnp.bfloat16)] * 7
         + [
             pltpu.SemaphoreType.DMA((src_count,)),
             pltpu.SemaphoreType.DMA((src_count,)),
@@ -214,10 +240,11 @@
             pltpu.SemaphoreType.DMA((2 * src_count,)),
             pltpu.SemaphoreType.DMA((2,)),
             pltpu.SemaphoreType.DMA((2,)),
-            pltpu.SemaphoreType.DMA((1,)),
+            pltpu.SemaphoreType.DMA((4,)),
         ],
         compiler_params=pltpu.CompilerParams(collective_id=0, has_side_effects=True),
     )(source, target, table)
+    return (src_read / src_total, tgt_read / tgt_total)
 
 
 def solution(mesh):

time: 49.3 us -> 50.1 us (1.016)
  other arithmetic: 0.03 us -> 4.02 us
  local copies, waits for them, and re-layouts: 5.36 us -> 2.59 us
    div x0 -> x2, other arithmetic: none -> 2.91 us  [on_device(): return (src_read / src_total, tgt_read / tgt_total)]
    unnamed x12, local copies, waits for them, and re-layouts: 4.7 us -> 1.96 us
    pallas_call x0 -> x2, other arithmetic: none -> 1.08 us  [on_device(): pl.pallas_call(functools.partial(kernel, feature_count, scaling), out_sha...]
where the time goes in v4:
time: 50.1 us; the launch traced here: 49.3 us
  Pallas kernels  42 us (84%)
  other arithmetic  4.02 us (8%)
  local copies, waits for them, and re-layouts  2.59 us (5%)
  between operations  0.7 us (1%)
    pallas_call x1, Pallas kernels, on_device(): pl.pallas_call(functools.partial(kernel, feature_count, scaling), out_sha...  42 us
    div x2, other arithmetic, on_device(): return (src_read / src_total, tgt_read / tgt_total)  2.91 us
    unnamed x12, local copies, waits for them, and re-layouts  1.96 us
    pallas_call x2, other arithmetic, on_device(): pl.pallas_call(functools.partial(kernel, feature_count, scaling), out_sha...  1.08 us

profile of v4, /device:TPU:1, one launch (start us, length us, event | category | flops | bytes accessed | tf_op | source)
XLA Modules:
  0.0 49.3 jit_solution(3330262512387128439)
XLA Ops:
  0.6 0.0 copy-start.5
  0.6 0.6 %copy-done.5 = s32[128]{0:T(128)S(1)} copy-done((s32[128]{0:T(128)S(1)}, s32[128]{0:T(128)}, u32[]{:S(2)}) %copy-start.5) | copy-done | bytes 536
  1.3 0.0 copy-start.3
  1.3 0.0 copy-start.4
  1.3 0.6 %copy-done.3 = s32[128]{0:T(128)S(1)} copy-done((s32[128]{0:T(128)S(1)}, s32[128]{0:T(128)}, u32[]{:S(2)}) %copy-start.3) | copy-done | bytes 536
  1.9 0.0 copy-done.4
  2.0 0.0 copy-start.2
  2.0 0.6 %copy-done.2 = s32[128]{0:T(128)S(1)} copy-done((s32[128]{0:T(128)S(1)}, s32[128]{0:T(128)}, u32[]{:S(2)}) %copy-start.2) | copy-done | bytes 536
  2.7 0.6 %pad.4.lab_hbm = f32[8,128]{1,0:T(8,128)} pad(f32[6,128]{1,0:T(8,128)S(1)} %convert_element_type.5, f32[]{:T(128)} %constant.65.clone.1), padding=0_2x0_0 | pad | bytes 7172 | tf_op jit(solution)/shard_map/jit(_pad)/pad | solution.py:218
  3.3 42.0 %shard_map.77 = (f32[128,1024]{1,0:T(8,128)}, f32[128,1024]{1,0:T(8,128)}, f32[128,1]{1,0:T(8,128)}, f32[128,1]{1,0:T(8,128)}) custom-call(bf16[128,1024]{1,0:T(8,128)(2,1)} %source_hbm.1, bf16[128,1024]{1,0:T(8,128)(2,1)} %target_hbm.1, f32[8,128]{1,0:T(8,128)} %pad.4.lab_hbm), custom_call_target="tpu_custom_call" | custom-call | tf_op jit(solution)/shard_map/pallas_call | solution.py:225
  45.3 0.0 copy-start.1
  45.3 1.0 %reduce = f32[128]{0:T(128)S(1)} reduce(f32[128,1]{1,0:T(8,128)} %get-tuple-element.7, f32[]{:T(128)} %constant.74), dimensions={1}, to_apply=%get-tuple-element.7.reduce_sub_computation | reduce | bytes 1028 | tf_op jit(solution)/shard_map/pallas_call | solution.py:225
  46.3 0.0 copy-done.1
  46.3 0.1 reduce.1
  46.4 0.0 copy-start
  46.4 2.0 %broadcast_divide_fusion = f32[128,1024]{1,0:T(8,128)} fusion(f32[128,1024]{1,0:T(8,128)} %get-tuple-element.8, f32[128]{0:T(128)S(1)} %reduce.1), kind=kLoop, calls=%fused_computation | loop fusion | flops 131072 | bytes 1049088 | tf_op jit(solution)/shard_map/div | solution.py:247
  48.4 0.0 copy-done
  48.4 0.9 %broadcast_divide_fusion.1 = f32[128,1024]{1,0:T(8,128)} fusion(f32[128,1024]{1,0:T(8,128)S(1)} %copy-done, f32[128]{0:T(128)S(1)} %reduce), kind=kLoop, calls=%fused_computation.1 | loop fusion | flops 131072 | bytes 1049088 | tf_op jit(solution)/shard_map/div | solution.py:247
  (4 shorter events, 0.1 us)
Async XLA Ops:
  0.6 0.7 %copy-start.5 = (s32[128]{0:T(128)S(1)}, s32[128]{0:T(128)}, u32[]{:S(2)}) copy-start(s32[128]{0:T(128)} %param.11) | copy-start | bytes 1540
  1.3 0.7 %copy-start.3 = (s32[128]{0:T(128)S(1)}, s32[128]{0:T(128)}, u32[]{:S(2)}) copy-start(s32[128]{0:T(128)} %param.8) | copy-start | bytes 1540
  1.3 0.7 %copy-start.4 = (s32[128]{0:T(128)S(1)}, s32[128]{0:T(128)}, u32[]{:S(2)}) copy-start(s32[128]{0:T(128)} %param.9) | copy-start | bytes 1540
  2.0 0.7 %copy-start.2 = (s32[128]{0:T(128)S(1)}, s32[128]{0:T(128)}, u32[]{:S(2)}) copy-start(s32[128]{0:T(128)} %param.10) | copy-start | bytes 1540
  45.3 1.0 %copy-start.1 = (f32[128,1]{1,0:T(8,128)S(1)}, f32[128,1]{1,0:T(8,128)}, u32[]{:S(2)}) copy-start(f32[128,1]{1,0:T(8,128)} %get-tuple-element.9) | copy-start | bytes 1540
  46.4 2.0 %copy-start = (f32[128,1024]{1,0:T(8,128)S(1)}, f32[128,1024]{1,0:T(8,128)}, u32[]{:S(2)}) copy-start(f32[128,1024]{1,0:T(8,128)} %get-tuple-element.6) | copy-start | bytes 1572868

commit v5 on v3

--- a/solution.py
+++ b/solution.py
@@ -12,7 +12,7 @@
 MESH = pl.DeviceIdType.MESH
 LABEL_LANES = 128
 DIGIT = 64
-SRC_HI, SRC_LO, SRC_BAND, DEST, TGT_HI, TGT_LO = range(6)
+SRC_HI, SRC_LO, SRC_BAND, TGT_HI, TGT_LO = 0, 1, 2, 4, 5
 
 
 def softmax_read(main, main_bucket, band_col, others, features, scaling, band_of_rows):
@@ -43,8 +43,14 @@
     return bucket, (slab[band:band + 1, :] if band is not None else None)
 
 
-def kernel(features, scaling, source, target, lab, src_out, tgt_out,
-           xsend, tsend, xs, xl, xr, tl, tr,
+def shift_of(divisor):
+    assert divisor & (divisor - 1) == 0
+    return divisor.bit_length() - 1
+
+
+def kernel(features, scaling, source_hbm, target_hbm, src_bucket_hbm, band_hbm, route_hbm,
+           tgt_bucket_hbm, src_out, tgt_out,
+           source, target, src_bucket, band, route, tgt_bucket, xsend, tsend, xs, xl, xr, tl, tr,
            a2a_send, a2a_recv, fw_send, fw_recv, nb_send, nb_recv, local_sem):
     g = lax.axis_index("src")
     t = lax.axis_index("tgt")
@@ -64,6 +70,12 @@
         offset = ((kz + 1) // 2) * (2 * (kz % 2) - 1)
         return ((z + offset + n_z) % n_z) * 2 + j % 2
 
+    pairs = ((source_hbm, source), (target_hbm, target), (src_bucket_hbm, src_bucket),
+             (band_hbm, band), (route_hbm, route), (tgt_bucket_hbm, tgt_bucket))
+    loads = [pltpu.make_async_copy(h, v, local_sem.at[1 + i]) for i, (h, v) in enumerate(pairs)]
+    for c in loads:
+        c.start()
+
     barrier = pltpu.get_barrier_semaphore()
     pl.semaphore_signal(barrier, inc=1, device_id=(partner, t), device_id_type=MESH)
 
@@ -75,16 +87,36 @@
     pl.semaphore_signal(barrier, inc=1, device_id=(g, left), device_id_type=MESH)
     pl.semaphore_signal(barrier, inc=1, device_id=(g, right), device_id_type=MESH)
 
-    table = lab[...]
-    labels = table.T.astype(jnp.bfloat16)
-    dest = table[DEST:DEST + 1, :].astype(jnp.int32)
-    onehot = (lax.broadcasted_iota(jnp.int32, (rows, rows), 0) == dest).astype(jnp.bfloat16)
+    for c in loads:
+        c.wait()
+
+    where_to = route[...]
+    dest = (where_to >> shift_of(rows * n_tgt)) * span + (where_to & ((1 << shift_of(span)) - 1))
+    sb = src_bucket[...]
+    tb = tgt_bucket[...]
+    label_rows_of = {
+        SRC_HI: sb >> shift_of(DIGIT), SRC_LO: sb & (DIGIT - 1), SRC_BAND: band[...],
+        TGT_HI: tb >> shift_of(DIGIT), TGT_LO: tb & (DIGIT - 1),
+    }
+    slot = lax.broadcasted_iota(jnp.int32, (rows, rows), 0)
+    lane = lax.broadcasted_iota(jnp.int32, (rows, LABEL_LANES), 1)
+    onehot = (slot == dest).astype(jnp.float32)
+    ident = (slot == lax.broadcasted_iota(jnp.int32, (rows, rows), 1)).astype(jnp.float32)
+
+    def label_slab(select, kinds):
+        slab = jnp.zeros((rows, LABEL_LANES), jnp.float32)
+        for k in kinds:
+            row = label_rows_of[k].astype(jnp.float32)
+            column = jnp.sum(select * row, axis=1, keepdims=True)
+            slab = jnp.where(lane == k, column, slab)
+        return slab.astype(jnp.bfloat16)
+
     xsend[:, :features] = jnp.dot(
-        onehot, source[...], preferred_element_type=jnp.float32).astype(jnp.bfloat16)
-    xsend[:, features:] = jnp.dot(
-        onehot, labels, preferred_element_type=jnp.float32).astype(jnp.bfloat16)
+        onehot.astype(jnp.bfloat16), source[...],
+        preferred_element_type=jnp.float32).astype(jnp.bfloat16)
+    xsend[:, features:] = label_slab(onehot, (SRC_HI, SRC_LO, SRC_BAND))
     tsend[:, :features] = target[...]
-    tsend[:, features:] = labels
+    tsend[:, features:] = label_slab(ident, (TGT_HI, TGT_LO))
 
     pl.semaphore_wait(barrier, n_src + 1)
 
@@ -107,14 +139,13 @@
 
     own = pltpu.make_async_copy(
         xsend.at[pl.ds(g * span, span)], xs.at[pl.ds(g * span, span)], local_sem.at[0])
+    def a2a_start(j, carry):
+        a2a_copy(far_peer(n_src - 3 - j), g).start()
+        return carry
+
+    lax.fori_loop(0, n_src - 2, a2a_start, 0)
+    a2a_copy(partner, g).start()
     own.start()
-    a2a_copy(partner, g).start()
-
-    def a2a_start(j, carry):
-        a2a_copy(far_peer(j), g).start()
-        return carry
-
-    lax.fori_loop(0, n_src - 2, a2a_start, 0)
 
     def forward(sender):
         rows_of = pl.ds(sender * span, span)
@@ -192,21 +223,19 @@
     per_peer = row_count // src_count
     scaling = 2.0 / math.sqrt(feature_count)
 
-    dest_slot = route // (row_count * tgt_count) * per_peer + route % per_peer
-    table = jnp.stack(
-        [src_bucket // DIGIT, src_bucket % DIGIT, band, dest_slot,
-         tgt_bucket // DIGIT, tgt_bucket % DIGIT]).astype(jnp.float32)
-    table = jnp.pad(table, ((0, LABEL_LANES - table.shape[0]), (0, 0)))
     width = feature_count + LABEL_LANES
+    ints = [v.reshape(1, row_count) for v in (src_bucket, band, route, tgt_bucket)]
 
     block = jax.ShapeDtypeStruct((row_count, feature_count), jnp.float32)
     vmem = pl.BlockSpec(memory_space=pltpu.VMEM)
     return pl.pallas_call(
         functools.partial(kernel, feature_count, scaling),
         out_shape=(block, block),
-        in_specs=[vmem, vmem, vmem],
+        in_specs=[pl.BlockSpec(memory_space=pl.ANY)] * 6,
         out_specs=(vmem, vmem),
-        scratch_shapes=[pltpu.VMEM((row_count, width), jnp.bfloat16)] * 7
+        scratch_shapes=[pltpu.VMEM((row_count, feature_count), jnp.bfloat16)] * 2
+        + [pltpu.VMEM((1, row_count), jnp.int32)] * 4
+        + [pltpu.VMEM((row_count, width), jnp.bfloat16)] * 7
         + [
             pltpu.SemaphoreType.DMA((src_count,)),
             pltpu.SemaphoreType.DMA((src_count,)),
@@ -214,10 +243,10 @@
             pltpu.SemaphoreType.DMA((2 * src_count,)),
             pltpu.SemaphoreType.DMA((2,)),
             pltpu.SemaphoreType.DMA((2,)),
-            pltpu.SemaphoreType.DMA((1,)),
+            pltpu.SemaphoreType.DMA((7,)),
         ],
         compiler_params=pltpu.CompilerParams(collective_id=0, has_side_effects=True),
-    )(source, target, table)
+    )(source, target, *ints)
 
 
 def solution(mesh):

time: 49.3 us -> 49.9 us (1.012); the launches traced: 48.5 us -> 49.7 us
  Pallas kernels: 42.5 us -> 46.3 us
  local copies, waits for them, and re-layouts: 5.36 us -> 2.74 us
    pallas_call x1, Pallas kernels: 42.5 us -> 46.3 us  [on_device(): pl.pallas_call(functools.partial(kernel, feature_count, scaling), out_sha...]
    unnamed x12 -> x4, local copies, waits for them, and re-layouts: 4.7 us -> 2.74 us
    pad x1 -> x0, local copies, waits for them, and re-layouts: 0.64 us -> none  [on_device(): table = jnp.pad(table, ((0, LABEL_LANES - table.shape[0]), (0, 0)))]
where the time goes in v5:
time: 49.9 us; the launch traced here: 49.7 us
  Pallas kernels  46.3 us (93%)
  local copies, waits for them, and re-layouts  2.74 us (5%)
  between operations  0.65 us (1%)
    pallas_call x1, Pallas kernels, on_device(): pl.pallas_call(functools.partial(kernel, feature_count, scaling), out_sha...  46.3 us
    unnamed x4, local copies, waits for them, and re-layouts  2.74 us

profile of v5, /device:TPU:1, one launch (start us, length us, event | category | flops | bytes accessed | tf_op | source)
XLA Modules:
  0.0 49.7 jit_solution(3793243966252759973)
XLA Ops:
  0.6 46.3 %shard_map.77 = (f32[128,1024]{1,0:T(8,128)}, f32[128,1024]{1,0:T(8,128)}) custom-call(bf16[128,1024]{1,0:T(8,128)(2,1)} %source_hbm.1, bf16[128,1024]{1,0:T(8,128)(2,1)} %target_hbm.1, s32[1,128]{1,0:T(1,128)} %bitcast.4, s32[1,128]{1,0:T(1,128)} %bitcast.5, s32[1,128]{1,0:T(1,128)} %bitcast.6, s32[1,128]{1,0:T(1,128)} %bitcast.7), custom_call_target="tpu_custom_call" | custom-call | tf_op jit(solution)/shard_map/pallas_call | solution.py:231
  47.0 0.0 copy-start
  47.0 1.9 %copy.10 = f32[128,1024]{1,0:T(8,128)} copy(f32[128,1024]{1,0:T(8,128)} %get-tuple-element.4) | data formatting | bytes 1048576
  48.9 0.0 copy-done
  48.9 0.8 %copy.11 = f32[128,1024]{1,0:T(8,128)} copy(f32[128,1024]{1,0:T(8,128)S(1)} %copy-done) | data formatting | bytes 1048576
Async XLA Ops:
  47.0 2.0 %copy-start = (f32[128,1024]{1,0:T(8,128)S(1)}, f32[128,1024]{1,0:T(8,128)}, u32[]{:S(2)}) copy-start(f32[128,1024]{1,0:T(8,128)} %get-tuple-element.5) | copy-start | bytes 1572868

commit v6 on v5

--- a/solution.py
+++ b/solution.py
@@ -50,8 +50,8 @@
 
 def kernel(features, scaling, source_hbm, target_hbm, src_bucket_hbm, band_hbm, route_hbm,
            tgt_bucket_hbm, src_out, tgt_out,
-           source, target, src_bucket, band, route, tgt_bucket, xsend, tsend, xs, xl, xr, tl, tr,
-           a2a_send, a2a_recv, fw_send, fw_recv, nb_send, nb_recv, local_sem):
+           source, target, src_bucket, band, route, tgt_bucket, xsend, tsend, xs, xp, xl, xr, tl, tr,
+           wsend, wrecv, fw_send, fw_recv, rsend, prelay, nb_send, nb_recv, local_sem):
     g = lax.axis_index("src")
     t = lax.axis_index("tgt")
     n_src = lax.axis_size("src")
@@ -65,11 +65,6 @@
     left = lax.rem(t + n_tgt - 1, n_tgt)
     right = lax.rem(t + 1, n_tgt)
 
-    def far_peer(j):
-        kz = j // 2 + 1
-        offset = ((kz + 1) // 2) * (2 * (kz % 2) - 1)
-        return ((z + offset + n_z) % n_z) * 2 + j % 2
-
     pairs = ((source_hbm, source), (target_hbm, target), (src_bucket_hbm, src_bucket),
              (band_hbm, band), (route_hbm, route), (tgt_bucket_hbm, tgt_bucket))
     loads = [pltpu.make_async_copy(h, v, local_sem.at[1 + i]) for i, (h, v) in enumerate(pairs)]
@@ -79,11 +74,16 @@
     barrier = pltpu.get_barrier_semaphore()
     pl.semaphore_signal(barrier, inc=1, device_id=(partner, t), device_id_type=MESH)
 
+    def z_far(j):
+        kz = j + 1
+        offset = ((kz + 1) // 2) * (2 * (kz % 2) - 1)
+        return (z + offset + n_z) % n_z
+
     def greet(j, carry):
-        pl.semaphore_signal(barrier, inc=1, device_id=(far_peer(j), t), device_id_type=MESH)
-        return carry
-
-    lax.fori_loop(0, n_src - 2, greet, 0)
+        pl.semaphore_signal(barrier, inc=1, device_id=(z_far(j) * 2 + core, t), device_id_type=MESH)
+        return carry
+
+    lax.fori_loop(0, n_z - 1, greet, 0)
     pl.semaphore_signal(barrier, inc=1, device_id=(g, left), device_id_type=MESH)
     pl.semaphore_signal(barrier, inc=1, device_id=(g, right), device_id_type=MESH)
 
@@ -118,7 +118,7 @@
     tsend[:, :features] = target[...]
     tsend[:, features:] = label_slab(ident, (TGT_HI, TGT_LO))
 
-    pl.semaphore_wait(barrier, n_src + 1)
+    pl.semaphore_wait(barrier, n_z + 2)
 
     t_to_right = pltpu.make_async_remote_copy(
         tsend, tl, nb_send.at[0], nb_recv.at[0], device_id=(g, right), device_id_type=MESH)
@@ -127,60 +127,82 @@
     t_to_right.start()
     t_to_left.start()
 
-    def a2a_copy(peer, sender):
+    wide = 2 * span
+    mine = core * span
+    theirs = (1 - core) * span
+
+    def wide_copy(zd, zs):
         return pltpu.make_async_remote_copy(
-            xsend.at[pl.ds(peer * span, span)],
-            xs.at[pl.ds(sender * span, span)],
-            a2a_send.at[peer],
-            a2a_recv.at[sender],
-            device_id=(peer, t),
-            device_id_type=MESH,
-        )
-
+            xsend.at[pl.ds(zd * wide, wide)], xs.at[pl.ds(zs * wide, wide)],
+            wsend.at[zd], wrecv.at[zs], device_id=(zd * 2 + core, t), device_id_type=MESH)
+
+    def relay_copy(zs):
+        return pltpu.make_async_remote_copy(
+            xs.at[pl.ds(zs * wide + theirs, span)], xp.at[pl.ds(zs * wide + mine, span)],
+            rsend.at[zs], prelay.at[zs], device_id=(partner, t), device_id_type=MESH)
+
+    def relay_arrival(zs):
+        return pltpu.make_async_remote_copy(
+            xs.at[pl.ds(zs * wide + mine, span)], xp.at[pl.ds(zs * wide + theirs, span)],
+            rsend.at[zs], prelay.at[zs], device_id=(partner, t), device_id_type=MESH)
+
+    def w_start(j, carry):
+        zd = z_far(n_z - 2 - j)
+        wide_copy(zd, z).start()
+        return carry
+
+    lax.fori_loop(0, n_z - 1, w_start, 0)
+    direct = pltpu.make_async_remote_copy(
+        xsend.at[pl.ds(z * wide + theirs, span)], xp.at[pl.ds(z * wide + mine, span)],
+        rsend.at[z], prelay.at[z], device_id=(partner, t), device_id_type=MESH)
+    direct.start()
     own = pltpu.make_async_copy(
-        xsend.at[pl.ds(g * span, span)], xs.at[pl.ds(g * span, span)], local_sem.at[0])
-    def a2a_start(j, carry):
-        a2a_copy(far_peer(n_src - 3 - j), g).start()
-        return carry
-
-    lax.fori_loop(0, n_src - 2, a2a_start, 0)
-    a2a_copy(partner, g).start()
+        xsend.at[pl.ds(z * wide + mine, span)], xs.at[pl.ds(z * wide + mine, span)], local_sem.at[0])
     own.start()
 
-    def forward(sender):
+    def forward(sender, buf):
         rows_of = pl.ds(sender * span, span)
         return (
             pltpu.make_async_remote_copy(
-                xs.at[rows_of], xl.at[rows_of], fw_send.at[sender], fw_recv.at[sender],
+                buf.at[rows_of], xl.at[rows_of], fw_send.at[sender], fw_recv.at[sender],
                 device_id=(g, right), device_id_type=MESH),
             pltpu.make_async_remote_copy(
-                xs.at[rows_of], xr.at[rows_of], fw_send.at[n_src + sender],
+                buf.at[rows_of], xr.at[rows_of], fw_send.at[n_src + sender],
                 fw_recv.at[n_src + sender], device_id=(g, left), device_id_type=MESH),
         )
 
-    def arrive_and_forward(sender):
-        rows_of = pl.ds(sender * span, span)
-        pltpu.make_async_remote_copy(
-            xsend.at[rows_of], xs.at[rows_of], a2a_send.at[sender], a2a_recv.at[sender],
-            device_id=(sender, t), device_id_type=MESH).wait_recv()
-        for c in forward(sender):
+    def wide_arrived(zs):
+        wide_copy(zs, zs).wait_recv()
+        relay_copy(zs).start()
+        for c in forward(zs * 2 + core, xs):
             c.start()
 
+    def relay_arrived(zs):
+        relay_arrival(zs).wait_recv()
+        for c in forward(zs * 2 + 1 - core, xp):
+            c.start()
+
     own.wait()
-    for c in forward(g):
+    for c in forward(g, xs):
         c.start()
-    arrive_and_forward(partner)
-
-    def a2a_arrive(j, carry):
-        arrive_and_forward(far_peer(j))
-        return carry
-
-    lax.fori_loop(0, n_src - 2, a2a_arrive, 0)
+    wide_arrived(z_far(0))
+
+    def w_arrive(j, carry):
+        wide_arrived(z_far(j))
+        relay_arrived(z_far(j - 1))
+        return carry
+
+    lax.fori_loop(1, n_z - 1, w_arrive, 0)
+    relay_arrived(z_far(n_z - 2))
+    relay_arrived(z)
 
     t_to_right.wait()
     t_to_left.wait()
 
-    x_cols = xs[:, features:].astype(jnp.float32).astype(jnp.int32)
+    sender_core = (lax.broadcasted_iota(jnp.int32, (rows, 1), 0) // span) % 2
+    merged = jnp.where(sender_core == core, xs[...], xp[...])
+
+    x_cols = merged[:, features:].astype(jnp.float32).astype(jnp.int32)
     x_bucket = x_cols[:, SRC_HI:SRC_HI + 1] * DIGIT + x_cols[:, SRC_LO:SRC_LO + 1]
     x_band = x_cols[:, SRC_BAND:SRC_BAND + 1]
     tgt_blocks = []
@@ -188,18 +210,18 @@
         bucket_row, _ = label_rows(blk[...], features, TGT_HI, TGT_LO)
         tgt_blocks.append((blk, bucket_row, None))
     src_out[...] = softmax_read(
-        xs[:, :features], x_bucket, x_band, tgt_blocks, features, scaling, True)
-
-    a2a_copy(partner, g).wait_send()
-
-    def a2a_sent(j, carry):
-        a2a_copy(far_peer(j), g).wait_send()
-        return carry
-
-    lax.fori_loop(0, n_src - 2, a2a_sent, 0)
+        merged[:, :features], x_bucket, x_band, tgt_blocks, features, scaling, True)
+
+    def w_sent(j, carry):
+        wide_copy(z_far(j), z).wait_send()
+        relay_copy(z_far(j)).wait_send()
+        return carry
+
+    lax.fori_loop(0, n_z - 1, w_sent, 0)
+    direct.wait_send()
 
     def fw_done(s, carry):
-        for c in forward(s):
+        for c in forward(s, xs):
             c.wait_send()
             c.wait_recv()
         return carry
@@ -209,7 +231,7 @@
     y_cols = tsend[:, features:].astype(jnp.float32).astype(jnp.int32)
     y_bucket = y_cols[:, TGT_HI:TGT_HI + 1] * DIGIT + y_cols[:, TGT_LO:TGT_LO + 1]
     src_blocks = []
-    for blk in (xl, xs, xr):
+    for blk in (xl, merged, xr):
         bucket_row, band_row = label_rows(blk[...], features, SRC_HI, SRC_LO, SRC_BAND)
         src_blocks.append((blk, bucket_row, band_row))
     tgt_out[...] = softmax_read(
@@ -235,12 +257,14 @@
         out_specs=(vmem, vmem),
         scratch_shapes=[pltpu.VMEM((row_count, feature_count), jnp.bfloat16)] * 2
         + [pltpu.VMEM((1, row_count), jnp.int32)] * 4
-        + [pltpu.VMEM((row_count, width), jnp.bfloat16)] * 7
+        + [pltpu.VMEM((row_count, width), jnp.bfloat16)] * 8
         + [
-            pltpu.SemaphoreType.DMA((src_count,)),
-            pltpu.SemaphoreType.DMA((src_count,)),
+            pltpu.SemaphoreType.DMA((src_count // 2,)),
+            pltpu.SemaphoreType.DMA((src_count // 2,)),
             pltpu.SemaphoreType.DMA((2 * src_count,)),
             pltpu.SemaphoreType.DMA((2 * src_count,)),
+            pltpu.SemaphoreType.DMA((src_count // 2,)),
+            pltpu.SemaphoreType.DMA((src_count // 2,)),
             pltpu.SemaphoreType.DMA((2,)),
             pltpu.SemaphoreType.DMA((2,)),
             pltpu.SemaphoreType.DMA((7,)),

time: 49.9 us -> 51 us (1.022)
  Pallas kernels: 46.3 us -> 47.5 us
    pallas_call x1, Pallas kernels: 46.3 us -> 47.5 us  [on_device(): pl.pallas_call(functools.partial(kernel, feature_count, scaling), out_sha...]
where the time goes in v6:
time: 51 us; the launch traced here: 50.9 us
  Pallas kernels  47.5 us (93%)
  local copies, waits for them, and re-layouts  2.74 us (5%)
  between operations  0.65 us (1%)
    pallas_call x1, Pallas kernels, on_device(): pl.pallas_call(functools.partial(kernel, feature_count, scaling), out_sha...  47.5 us
    unnamed x4, local copies, waits for them, and re-layouts  2.74 us

profile of v6, /device:TPU:1, one launch (start us, length us, event | category | flops | bytes accessed | tf_op | source)
XLA Modules:
  0.0 50.9 jit_solution(16779540198702997805)
XLA Ops:
  0.6 47.5 %shard_map.77 = (f32[128,1024]{1,0:T(8,128)}, f32[128,1024]{1,0:T(8,128)}) custom-call(bf16[128,1024]{1,0:T(8,128)(2,1)} %source_hbm.1, bf16[128,1024]{1,0:T(8,128)(2,1)} %target_hbm.1, s32[1,128]{1,0:T(1,128)} %bitcast.4, s32[1,128]{1,0:T(1,128)} %bitcast.5, s32[1,128]{1,0:T(1,128)} %bitcast.6, s32[1,128]{1,0:T(1,128)} %bitcast.7), custom_call_target="tpu_custom_call" | custom-call | tf_op jit(solution)/shard_map/pallas_call | solution.py:253
  48.1 0.0 copy-start
  48.1 1.9 %copy.10 = f32[128,1024]{1,0:T(8,128)} copy(f32[128,1024]{1,0:T(8,128)} %get-tuple-element.4) | data formatting | bytes 1048576
  50.1 0.0 copy-done
  50.1 0.8 %copy.11 = f32[128,1024]{1,0:T(8,128)} copy(f32[128,1024]{1,0:T(8,128)S(1)} %copy-done) | data formatting | bytes 1048576
Async XLA Ops:
  48.1 2.0 %copy-start = (f32[128,1024]{1,0:T(8,128)S(1)}, f32[128,1024]{1,0:T(8,128)}, u32[]{:S(2)}) copy-start(f32[128,1024]{1,0:T(8,128)} %get-tuple-element.5) | copy-start | bytes 1572868

commit v7 on v5

--- a/solution.py
+++ b/solution.py
@@ -139,13 +139,14 @@
 
     own = pltpu.make_async_copy(
         xsend.at[pl.ds(g * span, span)], xs.at[pl.ds(g * span, span)], local_sem.at[0])
+    own.start()
+    a2a_copy(partner, g).start()
+
     def a2a_start(j, carry):
-        a2a_copy(far_peer(n_src - 3 - j), g).start()
+        a2a_copy(far_peer(j), g).start()
         return carry
 
     lax.fori_loop(0, n_src - 2, a2a_start, 0)
-    a2a_copy(partner, g).start()
-    own.start()
 
     def forward(sender):
         rows_of = pl.ds(sender * span, span)

time: 49.9 us -> 46.2 us (0.926); the launches traced: 49.7 us -> 45.4 us
  Pallas kernels: 46.3 us -> 42 us
    pallas_call x1, Pallas kernels: 46.3 us -> 42 us  [on_device(): pl.pallas_call(functools.partial(kernel, feature_count, scaling), out_sha...]
where the time goes in v7:
time: 46.2 us; the launch traced here: 45.4 us
  Pallas kernels  42 us (91%)
  local copies, waits for them, and re-layouts  2.74 us (6%)
  between operations  0.65 us (1%)
    pallas_call x1, Pallas kernels, on_device(): pl.pallas_call(functools.partial(kernel, feature_count, scaling), out_sha...  42 us
    unnamed x4, local copies, waits for them, and re-layouts  2.74 us

profile of v7, /device:TPU:1, one launch (start us, length us, event | category | flops | bytes accessed | tf_op | source)
XLA Modules:
  0.0 45.4 jit_solution(15310794598660999125)
XLA Ops:
  0.6 42.0 %shard_map.77 = (f32[128,1024]{1,0:T(8,128)}, f32[128,1024]{1,0:T(8,128)}) custom-call(bf16[128,1024]{1,0:T(8,128)(2,1)} %source_hbm.1, bf16[128,1024]{1,0:T(8,128)(2,1)} %target_hbm.1, s32[1,128]{1,0:T(1,128)} %bitcast.4, s32[1,128]{1,0:T(1,128)} %bitcast.5, s32[1,128]{1,0:T(1,128)} %bitcast.6, s32[1,128]{1,0:T(1,128)} %bitcast.7), custom_call_target="tpu_custom_call" | custom-call | tf_op jit(solution)/shard_map/pallas_call | solution.py:232
  42.7 0.0 copy-start
  42.7 1.9 %copy.10 = f32[128,1024]{1,0:T(8,128)} copy(f32[128,1024]{1,0:T(8,128)} %get-tuple-element.4) | data formatting | bytes 1048576
  44.6 0.0 copy-done
  44.6 0.8 %copy.11 = f32[128,1024]{1,0:T(8,128)} copy(f32[128,1024]{1,0:T(8,128)S(1)} %copy-done) | data formatting | bytes 1048576
Async XLA Ops:
  42.7 2.0 %copy-start = (f32[128,1024]{1,0:T(8,128)S(1)}, f32[128,1024]{1,0:T(8,128)}, u32[]{:S(2)}) copy-start(f32[128,1024]{1,0:T(8,128)} %get-tuple-element.5) | copy-start | bytes 1572868

commit v8 on v7

--- a/solution.py
+++ b/solution.py
@@ -124,8 +124,6 @@
         tsend, tl, nb_send.at[0], nb_recv.at[0], device_id=(g, right), device_id_type=MESH)
     t_to_left = pltpu.make_async_remote_copy(
         tsend, tr, nb_send.at[1], nb_recv.at[1], device_id=(g, left), device_id_type=MESH)
-    t_to_right.start()
-    t_to_left.start()
 
     def a2a_copy(peer, sender):
         return pltpu.make_async_remote_copy(
@@ -147,6 +145,8 @@
         return carry
 
     lax.fori_loop(0, n_src - 2, a2a_start, 0)
+    t_to_right.start()
+    t_to_left.start()
 
     def forward(sender):
         rows_of = pl.ds(sender * span, span)

time: 46.2 us -> 46.2 us (level)
  no operation moved by 1% of the time
where the time goes in v8:
time: 46.2 us; the launch traced here: 45.4 us
  Pallas kernels  42 us (91%)
  local copies, waits for them, and re-layouts  2.74 us (6%)
  between operations  0.65 us (1%)
    pallas_call x1, Pallas kernels, on_device(): pl.pallas_call(functools.partial(kernel, feature_count, scaling), out_sha...  42 us
    unnamed x4, local copies, waits for them, and re-layouts  2.74 us

profile of v8, /device:TPU:1, one launch (start us, length us, event | category | flops | bytes accessed | tf_op | source)
XLA Modules:
  0.0 45.4 jit_solution(16738644256538249551)
XLA Ops:
  0.6 42.0 %shard_map.77 = (f32[128,1024]{1,0:T(8,128)}, f32[128,1024]{1,0:T(8,128)}) custom-call(bf16[128,1024]{1,0:T(8,128)(2,1)} %source_hbm.1, bf16[128,1024]{1,0:T(8,128)(2,1)} %target_hbm.1, s32[1,128]{1,0:T(1,128)} %bitcast.4, s32[1,128]{1,0:T(1,128)} %bitcast.5, s32[1,128]{1,0:T(1,128)} %bitcast.6, s32[1,128]{1,0:T(1,128)} %bitcast.7), custom_call_target="tpu_custom_call" | custom-call | tf_op jit(solution)/shard_map/pallas_call | solution.py:232
  42.7 0.0 copy-start
  42.7 1.9 %copy.10 = f32[128,1024]{1,0:T(8,128)} copy(f32[128,1024]{1,0:T(8,128)} %get-tuple-element.4) | data formatting | bytes 1048576
  44.6 0.0 copy-done
  44.6 0.8 %copy.11 = f32[128,1024]{1,0:T(8,128)} copy(f32[128,1024]{1,0:T(8,128)S(1)} %copy-done) | data formatting | bytes 1048576
Async XLA Ops:
  42.7 2.0 %copy-start = (f32[128,1024]{1,0:T(8,128)S(1)}, f32[128,1024]{1,0:T(8,128)}, u32[]{:S(2)}) copy-start(f32[128,1024]{1,0:T(8,128)} %get-tuple-element.5) | copy-start | bytes 1572868

commit v9 on v8

--- a/solution.py
+++ b/solution.py
@@ -77,15 +77,16 @@
         c.start()
 
     barrier = pltpu.get_barrier_semaphore()
-    pl.semaphore_signal(barrier, inc=1, device_id=(partner, t), device_id_type=MESH)
 
     def greet(j, carry):
-        pl.semaphore_signal(barrier, inc=1, device_id=(far_peer(j), t), device_id_type=MESH)
+        pl.semaphore_signal(
+            barrier, inc=1, device_id=(far_peer(n_src - 3 - j), t), device_id_type=MESH)
         return carry
 
     lax.fori_loop(0, n_src - 2, greet, 0)
     pl.semaphore_signal(barrier, inc=1, device_id=(g, left), device_id_type=MESH)
     pl.semaphore_signal(barrier, inc=1, device_id=(g, right), device_id_type=MESH)
+    pl.semaphore_signal(barrier, inc=1, device_id=(partner, t), device_id_type=MESH)
 
     for c in loads:
         c.wait()

time: 46.2 us -> 45.5 us (0.985); the launches traced: 45.4 us -> 45.3 us
  no operation moved by 1% of the time
where the time goes in v9:
time: 45.5 us; the launch traced here: 45.3 us
  Pallas kernels  42 us (92%)
  local copies, waits for them, and re-layouts  2.74 us (6%)
  between operations  0.65 us (1%)
    pallas_call x1, Pallas kernels, on_device(): pl.pallas_call(functools.partial(kernel, feature_count, scaling), out_sha...  42 us
    unnamed x4, local copies, waits for them, and re-layouts  2.74 us

profile of v9, /device:TPU:1, one launch (start us, length us, event | category | flops | bytes accessed | tf_op | source)
XLA Modules:
  0.0 45.3 jit_solution(13672503940562868165)
XLA Ops:
  0.6 42.0 %shard_map.77 = (f32[128,1024]{1,0:T(8,128)}, f32[128,1024]{1,0:T(8,128)}) custom-call(bf16[128,1024]{1,0:T(8,128)(2,1)} %source_hbm.1, bf16[128,1024]{1,0:T(8,128)(2,1)} %target_hbm.1, s32[1,128]{1,0:T(1,128)} %bitcast.4, s32[1,128]{1,0:T(1,128)} %bitcast.5, s32[1,128]{1,0:T(1,128)} %bitcast.6, s32[1,128]{1,0:T(1,128)} %bitcast.7), custom_call_target="tpu_custom_call" | custom-call | tf_op jit(solution)/shard_map/pallas_call | solution.py:233
  42.6 0.0 copy-start
  42.6 1.9 %copy.10 = f32[128,1024]{1,0:T(8,128)} copy(f32[128,1024]{1,0:T(8,128)} %get-tuple-element.4) | data formatting | bytes 1048576
  44.5 0.0 copy-done
  44.5 0.8 %copy.11 = f32[128,1024]{1,0:T(8,128)} copy(f32[128,1024]{1,0:T(8,128)S(1)} %copy-done) | data formatting | bytes 1048576
Async XLA Ops:
  42.6 2.0 %copy-start = (f32[128,1024]{1,0:T(8,128)S(1)}, f32[128,1024]{1,0:T(8,128)}, u32[]{:S(2)}) copy-start(f32[128,1024]{1,0:T(8,128)} %get-tuple-element.5) | copy-start | bytes 1572868

commit v10 on v9

--- a/solution.py
+++ b/solution.py
@@ -218,6 +218,26 @@
         tsend[:, :features], y_bucket, None, src_blocks, features, scaling, False)
 
 
+def write_kernel(src_in, tgt_in, src_res, tgt_res, sems):
+    copies = [pltpu.make_async_copy(src_in, src_res, sems.at[0]),
+              pltpu.make_async_copy(tgt_in, tgt_res, sems.at[1])]
+    for c in copies:
+        c.start()
+    for c in copies:
+        c.wait()
+
+
+def write_out(src_read, tgt_read):
+    return pl.pallas_call(
+        write_kernel,
+        out_shape=(jax.ShapeDtypeStruct(src_read.shape, src_read.dtype),
+                   jax.ShapeDtypeStruct(tgt_read.shape, tgt_read.dtype)),
+        in_specs=[pl.BlockSpec(memory_space=pltpu.VMEM)] * 2,
+        out_specs=(pl.BlockSpec(memory_space=pl.ANY),) * 2,
+        scratch_shapes=[pltpu.SemaphoreType.DMA((2,))],
+    )(src_read, tgt_read)
+
+
 def on_device(source, target, src_bucket, tgt_bucket, band, route):
     row_count, feature_count = source.shape
     src_count = lax.axis_size("src")
@@ -230,7 +250,7 @@
 
     block = jax.ShapeDtypeStruct((row_count, feature_count), jnp.float32)
     vmem = pl.BlockSpec(memory_space=pltpu.VMEM)
-    return pl.pallas_call(
+    reads = pl.pallas_call(
         functools.partial(kernel, feature_count, scaling),
         out_shape=(block, block),
         in_specs=[pl.BlockSpec(memory_space=pl.ANY)] * 6,
@@ -249,6 +269,7 @@
         ],
         compiler_params=pltpu.CompilerParams(collective_id=0, has_side_effects=True),
     )(source, target, *ints)
+    return write_out(*reads)
 
 
 def solution(mesh):

time: 45.5 us -> 44.9 us (0.987)
  local copies, waits for them, and re-layouts: 2.74 us -> 0 us
  Pallas kernels: 42 us -> 44.2 us
    unnamed x4 -> x0, local copies, waits for them, and re-layouts: 2.74 us -> none
    pallas_call x0 -> x1, Pallas kernels: none -> 2.18 us  [write_out(): pl.pallas_call(write_kernel, out_shape=(jax.ShapeDtypeStruct(src_read.sha...]
where the time goes in v10:
time: 44.9 us; the launch traced here: 44.8 us
  Pallas kernels  44.2 us (98%)
  between operations  0.64 us (1%)
    pallas_call x1, Pallas kernels, on_device(): pl.pallas_call(functools.partial(kernel, feature_count, scaling), out_sha...  42 us
    pallas_call x1, Pallas kernels, write_out(): pl.pallas_call(write_kernel, out_shape=(jax.ShapeDtypeStruct(src_read.sha...  2.18 us

profile of v10, /device:TPU:1, one launch (start us, length us, event | category | flops | bytes accessed | tf_op | source)
XLA Modules:
  0.0 44.8 jit_solution(1178827903836488039)
XLA Ops:
  0.6 42.0 %shard_map.77 = (f32[128,1024]{1,0:T(8,128)}, f32[128,1024]{1,0:T(8,128)}) custom-call(bf16[128,1024]{1,0:T(8,128)(2,1)} %source_hbm.1, bf16[128,1024]{1,0:T(8,128)(2,1)} %target_hbm.1, s32[1,128]{1,0:T(1,128)} %bitcast.4, s32[1,128]{1,0:T(1,128)} %bitcast.5, s32[1,128]{1,0:T(1,128)} %bitcast.6, s32[1,128]{1,0:T(1,128)} %bitcast.7), custom_call_target="tpu_custom_call" | custom-call | tf_op jit(solution)/shard_map/pallas_call | solution.py:253
  42.6 2.2 %shard_map.78 = (f32[128,1024]{1,0:T(8,128)}, f32[128,1024]{1,0:T(8,128)}) custom-call(f32[128,1024]{1,0:T(8,128)} %get-tuple-element.4.src_in, f32[128,1024]{1,0:T(8,128)} %get-tuple-element.5.tgt_in), custom_call_target="tpu_custom_call" | custom-call | tf_op jit(solution)/shard_map/pallas_call | solution.py:231

commit v11 on v10

--- a/solution.py
+++ b/solution.py
@@ -200,13 +200,12 @@
 
     lax.fori_loop(0, n_src - 2, a2a_sent, 0)
 
-    def fw_done(s, carry):
+    def fw_arrived(s, carry):
         for c in forward(s):
-            c.wait_send()
             c.wait_recv()
         return carry
 
-    lax.fori_loop(0, n_src, fw_done, 0)
+    lax.fori_loop(0, n_src, fw_arrived, 0)
 
     y_cols = tsend[:, features:].astype(jnp.float32).astype(jnp.int32)
     y_bucket = y_cols[:, TGT_HI:TGT_HI + 1] * DIGIT + y_cols[:, TGT_LO:TGT_LO + 1]
@@ -216,6 +215,13 @@
         src_blocks.append((blk, bucket_row, band_row))
     tgt_out[...] = softmax_read(
         tsend[:, :features], y_bucket, None, src_blocks, features, scaling, False)
+
+    def fw_sent(s, carry):
+        for c in forward(s):
+            c.wait_send()
+        return carry
+
+    lax.fori_loop(0, n_src, fw_sent, 0)
 
 
 def write_kernel(src_in, tgt_in, src_res, tgt_res, sems):

time: 44.9 us -> 45.3 us (level)
  no operation moved by 1% of the time
where the time goes in v11:
time: 45.3 us; the launch traced here: 45.2 us
  Pallas kernels  44.5 us (98%)
  between operations  0.64 us (1%)
    pallas_call x1, Pallas kernels, on_device(): pl.pallas_call(functools.partial(kernel, feature_count, scaling), out_sha...  42.4 us
    pallas_call x1, Pallas kernels, write_out(): pl.pallas_call(write_kernel, out_shape=(jax.ShapeDtypeStruct(src_read.sha...  2.18 us

profile of v11, /device:TPU:1, one launch (start us, length us, event | category | flops | bytes accessed | tf_op | source)
XLA Modules:
  0.0 45.2 jit_solution(10334000716547959166)
XLA Ops:
  0.6 42.4 %shard_map.77 = (f32[128,1024]{1,0:T(8,128)}, f32[128,1024]{1,0:T(8,128)}) custom-call(bf16[128,1024]{1,0:T(8,128)(2,1)} %source_hbm.1, bf16[128,1024]{1,0:T(8,128)(2,1)} %target_hbm.1, s32[1,128]{1,0:T(1,128)} %bitcast.4, s32[1,128]{1,0:T(1,128)} %bitcast.5, s32[1,128]{1,0:T(1,128)} %bitcast.6, s32[1,128]{1,0:T(1,128)} %bitcast.7), custom_call_target="tpu_custom_call" | custom-call | tf_op jit(solution)/shard_map/pallas_call | solution.py:259
  43.0 2.2 %shard_map.78 = (f32[128,1024]{1,0:T(8,128)}, f32[128,1024]{1,0:T(8,128)}) custom-call(f32[128,1024]{1,0:T(8,128)} %get-tuple-element.4.src_in, f32[128,1024]{1,0:T(8,128)} %get-tuple-element.5.tgt_in), custom_call_target="tpu_custom_call" | custom-call | tf_op jit(solution)/shard_map/pallas_call | solution.py:237

commit v12 on v11

--- a/solution.py
+++ b/solution.py
@@ -15,21 +15,21 @@
 SRC_HI, SRC_LO, SRC_BAND, TGT_HI, TGT_LO = 0, 1, 2, 4, 5
 
 
-def softmax_read(main, main_bucket, band_col, others, features, scaling, band_of_rows):
-    scores, masks = [], []
-    for blk, bucket_row, band_row in others:
-        s = lax.dot_general(
-            main, blk[:, :features], (((1,), (1,)), ((), ())),
-            preferred_element_type=jnp.float32) * scaling
-        band = band_col if band_of_rows else band_row
-        ok = (jnp.abs(main_bucket - bucket_row) <= band) & (
-            (main_bucket >> 7) == (bucket_row >> 7))
-        scores.append(jnp.where(ok, s, lowest))
-        masks.append(ok)
-    top = functools.reduce(jnp.maximum, [jnp.max(s, axis=1, keepdims=True) for s in scores])
+def masked_scores(main, main_bucket, band_col, blk, bucket_row, band_row, features, scaling):
+    s = lax.dot_general(
+        main, blk[:, :features], (((1,), (1,)), ((), ())),
+        preferred_element_type=jnp.float32) * scaling
+    band = band_col if band_row is None else band_row
+    ok = (jnp.abs(main_bucket - bucket_row) <= band) & (
+        (main_bucket >> 7) == (bucket_row >> 7))
+    return jnp.where(ok, s, lowest), ok
+
+
+def softmax_finish(scored, features):
+    top = functools.reduce(jnp.maximum, [jnp.max(s, axis=1, keepdims=True) for s, _, _ in scored])
     total = jnp.zeros_like(top)
-    read = jnp.zeros((main.shape[0], features), jnp.float32)
-    for s, ok, (blk, _, _) in zip(scores, masks, others):
+    read = jnp.zeros((top.shape[0], features), jnp.float32)
+    for s, ok, blk in scored:
         w = jnp.where(ok, jnp.exp(s - top), 0.0)
         total = total + jnp.sum(w, axis=1, keepdims=True)
         read = read + jnp.dot(w.astype(jnp.bfloat16), blk[:, :features],
@@ -185,12 +185,24 @@
     x_cols = xs[:, features:].astype(jnp.float32).astype(jnp.int32)
     x_bucket = x_cols[:, SRC_HI:SRC_HI + 1] * DIGIT + x_cols[:, SRC_LO:SRC_LO + 1]
     x_band = x_cols[:, SRC_BAND:SRC_BAND + 1]
-    tgt_blocks = []
+    row_scored = []
     for blk in (tl, tsend, tr):
         bucket_row, _ = label_rows(blk[...], features, TGT_HI, TGT_LO)
-        tgt_blocks.append((blk, bucket_row, None))
-    src_out[...] = softmax_read(
-        xs[:, :features], x_bucket, x_band, tgt_blocks, features, scaling, True)
+        s, ok = masked_scores(xs[:, :features], x_bucket, x_band, blk, bucket_row, None,
+                              features, scaling)
+        row_scored.append((s, ok, blk))
+    src_out[...] = softmax_finish(row_scored, features)
+
+    y_cols = tsend[:, features:].astype(jnp.float32).astype(jnp.int32)
+    y_bucket = y_cols[:, TGT_HI:TGT_HI + 1] * DIGIT + y_cols[:, TGT_LO:TGT_LO + 1]
+
+    def col_scored(blk):
+        bucket_row, band_row = label_rows(blk[...], features, SRC_HI, SRC_LO, SRC_BAND)
+        s, ok = masked_scores(tsend[:, :features], y_bucket, None, blk, bucket_row, band_row,
+                              features, scaling)
+        return (s, ok, blk)
+
+    own_scored = col_scored(xs)
 
     a2a_copy(partner, g).wait_send()
 
@@ -200,21 +212,19 @@
 
     lax.fori_loop(0, n_src - 2, a2a_sent, 0)
 
-    def fw_arrived(s, carry):
-        for c in forward(s):
-            c.wait_recv()
-        return carry
-
-    lax.fori_loop(0, n_src, fw_arrived, 0)
-
-    y_cols = tsend[:, features:].astype(jnp.float32).astype(jnp.int32)
-    y_bucket = y_cols[:, TGT_HI:TGT_HI + 1] * DIGIT + y_cols[:, TGT_LO:TGT_LO + 1]
-    src_blocks = []
-    for blk in (xl, xs, xr):
-        bucket_row, band_row = label_rows(blk[...], features, SRC_HI, SRC_LO, SRC_BAND)
-        src_blocks.append((blk, bucket_row, band_row))
-    tgt_out[...] = softmax_read(
-        tsend[:, :features], y_bucket, None, src_blocks, features, scaling, False)
+    def left_arrived(s, carry):
+        forward(s)[0].wait_recv()
+        return carry
+
+    def right_arrived(s, carry):
+        forward(s)[1].wait_recv()
+        return carry
+
+    lax.fori_loop(0, n_src, left_arrived, 0)
+    left_scored = col_scored(xl)
+    lax.fori_loop(0, n_src, right_arrived, 0)
+    right_scored = col_scored(xr)
+    tgt_out[...] = softmax_finish([left_scored, own_scored, right_scored], features)
 
     def fw_sent(s, carry):
         for c in forward(s):

time: 45.3 us -> 45.5 us (level)
  no operation moved by 1% of the time
where the time goes in v12:
time: 45.5 us; the launch traced here: 45.4 us
  Pallas kernels  44.7 us (98%)
  between operations  0.64 us (1%)
    pallas_call x1, Pallas kernels, on_device(): pl.pallas_call(functools.partial(kernel, feature_count, scaling), out_sha...  42.5 us
    pallas_call x1, Pallas kernels, write_out(): pl.pallas_call(write_kernel, out_shape=(jax.ShapeDtypeStruct(src_read.sha...  2.18 us

profile of v12, /device:TPU:1, one launch (start us, length us, event | category | flops | bytes accessed | tf_op | source)
XLA Modules:
  0.0 45.4 jit_solution(2875897955336950566)
XLA Ops:
  0.6 42.5 %shard_map.77 = (f32[128,1024]{1,0:T(8,128)}, f32[128,1024]{1,0:T(8,128)}) custom-call(bf16[128,1024]{1,0:T(8,128)(2,1)} %source_hbm.1, bf16[128,1024]{1,0:T(8,128)(2,1)} %target_hbm.1, s32[1,128]{1,0:T(1,128)} %bitcast.4, s32[1,128]{1,0:T(1,128)} %bitcast.5, s32[1,128]{1,0:T(1,128)} %bitcast.6, s32[1,128]{1,0:T(1,128)} %bitcast.7), custom_call_target="tpu_custom_call" | custom-call | tf_op jit(solution)/shard_map/pallas_call | solution.py:269
  43.2 2.2 %shard_map.78 = (f32[128,1024]{1,0:T(8,128)}, f32[128,1024]{1,0:T(8,128)}) custom-call(f32[128,1024]{1,0:T(8,128)} %get-tuple-element.4.src_in, f32[128,1024]{1,0:T(8,128)} %get-tuple-element.5.tgt_in), custom_call_target="tpu_custom_call" | custom-call | tf_op jit(solution)/shard_map/pallas_call | solution.py:247

commit v13 on v10

--- a/solution.py
+++ b/solution.py
@@ -72,10 +72,6 @@
 
     pairs = ((source_hbm, source), (target_hbm, target), (src_bucket_hbm, src_bucket),
              (band_hbm, band), (route_hbm, route), (tgt_bucket_hbm, tgt_bucket))
-    loads = [pltpu.make_async_copy(h, v, local_sem.at[1 + i]) for i, (h, v) in enumerate(pairs)]
-    for c in loads:
-        c.start()
-
     barrier = pltpu.get_barrier_semaphore()
 
     def greet(j, carry):
@@ -88,6 +84,9 @@
     pl.semaphore_signal(barrier, inc=1, device_id=(g, right), device_id_type=MESH)
     pl.semaphore_signal(barrier, inc=1, device_id=(partner, t), device_id_type=MESH)
 
+    loads = [pltpu.make_async_copy(h, v, local_sem.at[1 + i]) for i, (h, v) in enumerate(pairs)]
+    for c in loads:
+        c.start()
     for c in loads:
         c.wait()
 

time: 44.9 us -> 45 us (level)
  no operation moved by 1% of the time
where the time goes in v13:
time: 45 us; the launch traced here: 44.8 us
  Pallas kernels  44.2 us (98%)
  between operations  0.64 us (1%)
    pallas_call x1, Pallas kernels, on_device(): pl.pallas_call(functools.partial(kernel, feature_count, scaling), out_sha...  42 us
    pallas_call x1, Pallas kernels, write_out(): pl.pallas_call(write_kernel, out_shape=(jax.ShapeDtypeStruct(src_read.sha...  2.18 us

profile of v13, /device:TPU:1, one launch (start us, length us, event | category | flops | bytes accessed | tf_op | source)
XLA Modules:
  0.0 44.8 jit_solution(14610639774182951342)
XLA Ops:
  0.6 42.0 %shard_map.77 = (f32[128,1024]{1,0:T(8,128)}, f32[128,1024]{1,0:T(8,128)}) custom-call(bf16[128,1024]{1,0:T(8,128)(2,1)} %source_hbm.1, bf16[128,1024]{1,0:T(8,128)(2,1)} %target_hbm.1, s32[1,128]{1,0:T(1,128)} %bitcast.4, s32[1,128]{1,0:T(1,128)} %bitcast.5, s32[1,128]{1,0:T(1,128)} %bitcast.6, s32[1,128]{1,0:T(1,128)} %bitcast.7), custom_call_target="tpu_custom_call" | custom-call | tf_op jit(solution)/shard_map/pallas_call | solution.py:252
  42.6 2.2 %shard_map.78 = (f32[128,1024]{1,0:T(8,128)}, f32[128,1024]{1,0:T(8,128)}) custom-call(f32[128,1024]{1,0:T(8,128)} %get-tuple-element.4.src_in, f32[128,1024]{1,0:T(8,128)} %get-tuple-element.5.tgt_in), custom_call_target="tpu_custom_call" | custom-call | tf_op jit(solution)/shard_map/pallas_call | solution.py:230

commit v14 on v13

--- a/solution.py
+++ b/solution.py
@@ -68,18 +68,16 @@
     def far_peer(j):
         kz = j // 2 + 1
         offset = ((kz + 1) // 2) * (2 * (kz % 2) - 1)
-        return ((z + offset + n_z) % n_z) * 2 + j % 2
+        return ((z + offset + n_z) & (n_z - 1)) * 2 + j % 2
+
+    shift_of(n_z)
 
     pairs = ((source_hbm, source), (target_hbm, target), (src_bucket_hbm, src_bucket),
              (band_hbm, band), (route_hbm, route), (tgt_bucket_hbm, tgt_bucket))
     barrier = pltpu.get_barrier_semaphore()
 
-    def greet(j, carry):
-        pl.semaphore_signal(
-            barrier, inc=1, device_id=(far_peer(n_src - 3 - j), t), device_id_type=MESH)
-        return carry
-
-    lax.fori_loop(0, n_src - 2, greet, 0)
+    for j in range(n_src - 3, -1, -1):
+        pl.semaphore_signal(barrier, inc=1, device_id=(far_peer(j), t), device_id_type=MESH)
     pl.semaphore_signal(barrier, inc=1, device_id=(g, left), device_id_type=MESH)
     pl.semaphore_signal(barrier, inc=1, device_id=(g, right), device_id_type=MESH)
     pl.semaphore_signal(barrier, inc=1, device_id=(partner, t), device_id_type=MESH)
@@ -140,11 +138,8 @@
     own.start()
     a2a_copy(partner, g).start()
 
-    def a2a_start(j, carry):
+    for j in range(n_src - 2):
         a2a_copy(far_peer(j), g).start()
-        return carry
-
-    lax.fori_loop(0, n_src - 2, a2a_start, 0)
     t_to_right.start()
     t_to_left.start()
 
@@ -172,11 +167,8 @@
         c.start()
     arrive_and_forward(partner)
 
-    def a2a_arrive(j, carry):
+    for j in range(n_src - 2):
         arrive_and_forward(far_peer(j))
-        return carry
-
-    lax.fori_loop(0, n_src - 2, a2a_arrive, 0)
 
     t_to_right.wait()
     t_to_left.wait()

time: 45 us -> 44.6 us (level)
  no operation moved by 1% of the time
where the time goes in v14:
time: 44.6 us; the launch traced here: 44.5 us
  Pallas kernels  43.8 us (98%)
  between operations  0.64 us (1%)
    pallas_call x1, Pallas kernels, on_device(): pl.pallas_call(functools.partial(kernel, feature_count, scaling), out_sha...  41.7 us
    pallas_call x1, Pallas kernels, write_out(): pl.pallas_call(write_kernel, out_shape=(jax.ShapeDtypeStruct(src_read.sha...  2.18 us

profile of v14, /device:TPU:1, one launch (start us, length us, event | category | flops | bytes accessed | tf_op | source)
XLA Modules:
  0.0 44.5 jit_solution(9550463739855816726)
XLA Ops:
  0.6 41.7 %shard_map.77 = (f32[128,1024]{1,0:T(8,128)}, f32[128,1024]{1,0:T(8,128)}) custom-call(bf16[128,1024]{1,0:T(8,128)(2,1)} %source_hbm.1, bf16[128,1024]{1,0:T(8,128)(2,1)} %target_hbm.1, s32[1,128]{1,0:T(1,128)} %bitcast.4, s32[1,128]{1,0:T(1,128)} %bitcast.5, s32[1,128]{1,0:T(1,128)} %bitcast.6, s32[1,128]{1,0:T(1,128)} %bitcast.7), custom_call_target="tpu_custom_call" | custom-call | tf_op jit(solution)/shard_map/pallas_call | solution.py:244
  42.3 2.2 %shard_map.78 = (f32[128,1024]{1,0:T(8,128)}, f32[128,1024]{1,0:T(8,128)}) custom-call(f32[128,1024]{1,0:T(8,128)} %get-tuple-element.4.src_in, f32[128,1024]{1,0:T(8,128)} %get-tuple-element.5.tgt_in), custom_call_target="tpu_custom_call" | custom-call | tf_op jit(solution)/shard_map/pallas_call | solution.py:222

commit v15 on v14

--- a/solution.py
+++ b/solution.py
@@ -183,21 +183,12 @@
     src_out[...] = softmax_read(
         xs[:, :features], x_bucket, x_band, tgt_blocks, features, scaling, True)
 
-    a2a_copy(partner, g).wait_send()
-
-    def a2a_sent(j, carry):
-        a2a_copy(far_peer(j), g).wait_send()
-        return carry
-
-    lax.fori_loop(0, n_src - 2, a2a_sent, 0)
-
-    def fw_done(s, carry):
+    def fw_arrived(s, carry):
         for c in forward(s):
-            c.wait_send()
             c.wait_recv()
         return carry
 
-    lax.fori_loop(0, n_src, fw_done, 0)
+    lax.fori_loop(0, n_src, fw_arrived, 0)
 
     y_cols = tsend[:, features:].astype(jnp.float32).astype(jnp.int32)
     y_bucket = y_cols[:, TGT_HI:TGT_HI + 1] * DIGIT + y_cols[:, TGT_LO:TGT_LO + 1]
@@ -207,6 +198,21 @@
         src_blocks.append((blk, bucket_row, band_row))
     tgt_out[...] = softmax_read(
         tsend[:, :features], y_bucket, None, src_blocks, features, scaling, False)
+
+    a2a_copy(partner, g).wait_send()
+
+    def a2a_sent(j, carry):
+        a2a_copy(far_peer(j), g).wait_send()
+        return carry
+
+    lax.fori_loop(0, n_src - 2, a2a_sent, 0)
+
+    def fw_sent(s, carry):
+        for c in forward(s):
+            c.wait_send()
+        return carry
+
+    lax.fori_loop(0, n_src, fw_sent, 0)
 
 
 def write_kernel(src_in, tgt_in, src_res, tgt_res, sems):

time: 44.6 us -> 45.8 us (1.027)
  Pallas kernels: 43.8 us -> 45 us
    pallas_call x1, Pallas kernels: 41.7 us -> 42.8 us  [on_device(): pl.pallas_call(functools.partial(kernel, feature_count, scaling), out_sha...]
where the time goes in v15:
time: 45.8 us; the launch traced here: 45.6 us
  Pallas kernels  45 us (98%)
  between operations  0.64 us (1%)
    pallas_call x1, Pallas kernels, on_device(): pl.pallas_call(functools.partial(kernel, feature_count, scaling), out_sha...  42.8 us
    pallas_call x1, Pallas kernels, write_out(): pl.pallas_call(write_kernel, out_shape=(jax.ShapeDtypeStruct(src_read.sha...  2.18 us

profile of v15, /device:TPU:1, one launch (start us, length us, event | category | flops | bytes accessed | tf_op | source)
XLA Modules:
  0.0 45.6 jit_solution(2153001647211716997)
XLA Ops:
  0.6 42.8 %shard_map.77 = (f32[128,1024]{1,0:T(8,128)}, f32[128,1024]{1,0:T(8,128)}) custom-call(bf16[128,1024]{1,0:T(8,128)(2,1)} %source_hbm.1, bf16[128,1024]{1,0:T(8,128)(2,1)} %target_hbm.1, s32[1,128]{1,0:T(1,128)} %bitcast.4, s32[1,128]{1,0:T(1,128)} %bitcast.5, s32[1,128]{1,0:T(1,128)} %bitcast.6, s32[1,128]{1,0:T(1,128)} %bitcast.7), custom_call_target="tpu_custom_call" | custom-call | tf_op jit(solution)/shard_map/pallas_call | solution.py:250
  43.5 2.2 %shard_map.78 = (f32[128,1024]{1,0:T(8,128)}, f32[128,1024]{1,0:T(8,128)}) custom-call(f32[128,1024]{1,0:T(8,128)} %get-tuple-element.4.src_in, f32[128,1024]{1,0:T(8,128)} %get-tuple-element.5.tgt_in), custom_call_target="tpu_custom_call" | custom-call | tf_op jit(solution)/shard_map/pallas_call | solution.py:228

commit v16 on v14

--- a/solution.py
+++ b/solution.py
@@ -185,11 +185,8 @@
 
     a2a_copy(partner, g).wait_send()
 
-    def a2a_sent(j, carry):
+    for j in range(n_src - 2):
         a2a_copy(far_peer(j), g).wait_send()
-        return carry
-
-    lax.fori_loop(0, n_src - 2, a2a_sent, 0)
 
     def fw_done(s, carry):
         for c in forward(s):

time: 44.6 us -> 44.6 us (level)
  no operation moved by 1% of the time
where the time goes in v16:
time: 44.6 us; the launch traced here: 44.5 us
  Pallas kernels  43.8 us (98%)
  between operations  0.64 us (1%)
    pallas_call x1, Pallas kernels, on_device(): pl.pallas_call(functools.partial(kernel, feature_count, scaling), out_sha...  41.7 us
    pallas_call x1, Pallas kernels, write_out(): pl.pallas_call(write_kernel, out_shape=(jax.ShapeDtypeStruct(src_read.sha...  2.18 us

profile of v16, /device:TPU:1, one launch (start us, length us, event | category | flops | bytes accessed | tf_op | source)
XLA Modules:
  0.0 44.5 jit_solution(12379119869127338623)
XLA Ops:
  0.6 41.7 %shard_map.77 = (f32[128,1024]{1,0:T(8,128)}, f32[128,1024]{1,0:T(8,128)}) custom-call(bf16[128,1024]{1,0:T(8,128)(2,1)} %source_hbm.1, bf16[128,1024]{1,0:T(8,128)(2,1)} %target_hbm.1, s32[1,128]{1,0:T(1,128)} %bitcast.4, s32[1,128]{1,0:T(1,128)} %bitcast.5, s32[1,128]{1,0:T(1,128)} %bitcast.6, s32[1,128]{1,0:T(1,128)} %bitcast.7), custom_call_target="tpu_custom_call" | custom-call | tf_op jit(solution)/shard_map/pallas_call | solution.py:241
  42.3 2.2 %shard_map.78 = (f32[128,1024]{1,0:T(8,128)}, f32[128,1024]{1,0:T(8,128)}) custom-call(f32[128,1024]{1,0:T(8,128)} %get-tuple-element.4.src_in, f32[128,1024]{1,0:T(8,128)} %get-tuple-element.5.tgt_in), custom_call_target="tpu_custom_call" | custom-call | tf_op jit(solution)/shard_map/pallas_call | solution.py:219

commit v17 on v14

--- a/solution.py
+++ b/solution.py
@@ -138,8 +138,13 @@
     own.start()
     a2a_copy(partner, g).start()
 
+    def mirrored_peer(j):
+        kz = j // 2 + 1
+        offset = ((kz + 1) // 2) * (2 * (kz % 2) - 1)
+        return ((z + offset * (1 - 2 * core) + n_z) & (n_z - 1)) * 2 + j % 2
+
     for j in range(n_src - 2):
-        a2a_copy(far_peer(j), g).start()
+        a2a_copy(mirrored_peer(j), g).start()
     t_to_right.start()
     t_to_left.start()
 

time: 44.6 us -> 44.6 us (level)
  no operation moved by 1% of the time
where the time goes in v17:
time: 44.6 us; the launch traced here: 44.5 us
  Pallas kernels  43.8 us (98%)
  between operations  0.64 us (1%)
    pallas_call x1, Pallas kernels, on_device(): pl.pallas_call(functools.partial(kernel, feature_count, scaling), out_sha...  41.7 us
    pallas_call x1, Pallas kernels, write_out(): pl.pallas_call(write_kernel, out_shape=(jax.ShapeDtypeStruct(src_read.sha...  2.18 us

profile of v17, /device:TPU:1, one launch (start us, length us, event | category | flops | bytes accessed | tf_op | source)
XLA Modules:
  0.0 44.5 jit_solution(281242693842597289)
XLA Ops:
  0.6 41.7 %shard_map.77 = (f32[128,1024]{1,0:T(8,128)}, f32[128,1024]{1,0:T(8,128)}) custom-call(bf16[128,1024]{1,0:T(8,128)(2,1)} %source_hbm.1, bf16[128,1024]{1,0:T(8,128)(2,1)} %target_hbm.1, s32[1,128]{1,0:T(1,128)} %bitcast.4, s32[1,128]{1,0:T(1,128)} %bitcast.5, s32[1,128]{1,0:T(1,128)} %bitcast.6, s32[1,128]{1,0:T(1,128)} %bitcast.7), custom_call_target="tpu_custom_call" | custom-call | tf_op jit(solution)/shard_map/pallas_call | solution.py:249
  42.3 2.2 %shard_map.78 = (f32[128,1024]{1,0:T(8,128)}, f32[128,1024]{1,0:T(8,128)}) custom-call(f32[128,1024]{1,0:T(8,128)} %get-tuple-element.4.src_in, f32[128,1024]{1,0:T(8,128)} %get-tuple-element.5.tgt_in), custom_call_target="tpu_custom_call" | custom-call | tf_op jit(solution)/shard_map/pallas_call | solution.py:227

commit v18 on v14

--- a/solution.py
+++ b/solution.py
@@ -209,23 +209,21 @@
         tsend[:, :features], y_bucket, None, src_blocks, features, scaling, False)
 
 
-def write_kernel(src_in, tgt_in, src_res, tgt_res, sems):
-    copies = [pltpu.make_async_copy(src_in, src_res, sems.at[0]),
-              pltpu.make_async_copy(tgt_in, tgt_res, sems.at[1])]
-    for c in copies:
-        c.start()
-    for c in copies:
-        c.wait()
-
-
-def write_out(src_read, tgt_read):
+def write_kernel(src_in, tgt_in, src_res, tgt_res):
+    src_res[...] = src_in[...]
+    tgt_res[...] = tgt_in[...]
+
+
+def write_out(src_read, tgt_read, steps=4):
+    rows, columns = src_read.shape
+    spec = pl.BlockSpec((rows // steps, columns), lambda i: (i, 0))
     return pl.pallas_call(
         write_kernel,
+        grid=(steps,),
         out_shape=(jax.ShapeDtypeStruct(src_read.shape, src_read.dtype),
                    jax.ShapeDtypeStruct(tgt_read.shape, tgt_read.dtype)),
-        in_specs=[pl.BlockSpec(memory_space=pltpu.VMEM)] * 2,
-        out_specs=(pl.BlockSpec(memory_space=pl.ANY),) * 2,
-        scratch_shapes=[pltpu.SemaphoreType.DMA((2,))],
+        in_specs=[spec, spec],
+        out_specs=(spec, spec),
     )(src_read, tgt_read)
 
 

time: 44.6 us -> 45.9 us (1.029)
  Pallas kernels: 43.8 us -> 45.1 us
    pallas_call x1, Pallas kernels: 2.18 us -> 3.41 us  [write_out(): pl.pallas_call(write_kernel, grid=(steps,), out_shape=(jax.ShapeDtypeStru...]
where the time goes in v18:
time: 45.9 us; the launch traced here: 45.7 us
  Pallas kernels  45.1 us (98%)
  between operations  0.64 us (1%)
    pallas_call x1, Pallas kernels, on_device(): pl.pallas_call(functools.partial(kernel, feature_count, scaling), out_sha...  41.7 us
    pallas_call x1, Pallas kernels, write_out(): pl.pallas_call(write_kernel, grid=(steps,), out_shape=(jax.ShapeDtypeStru...  3.41 us

profile of v18, /device:TPU:1, one launch (start us, length us, event | category | flops | bytes accessed | tf_op | source)
XLA Modules:
  0.0 45.7 jit_solution(4295184559945168534)
XLA Ops:
  0.6 41.7 %shard_map.77 = (f32[128,1024]{1,0:T(8,128)}, f32[128,1024]{1,0:T(8,128)}) custom-call(bf16[128,1024]{1,0:T(8,128)(2,1)} %source_hbm.1, bf16[128,1024]{1,0:T(8,128)(2,1)} %target_hbm.1, s32[1,128]{1,0:T(1,128)} %bitcast.4, s32[1,128]{1,0:T(1,128)} %bitcast.5, s32[1,128]{1,0:T(1,128)} %bitcast.6, s32[1,128]{1,0:T(1,128)} %bitcast.7), custom_call_target="tpu_custom_call" | custom-call | tf_op jit(solution)/shard_map/pallas_call | solution.py:242
  42.3 3.4 %shard_map.78 = (f32[128,1024]{1,0:T(8,128)}, f32[128,1024]{1,0:T(8,128)}) custom-call(f32[128,1024]{1,0:T(8,128)} %get-tuple-element.4.src_in, f32[128,1024]{1,0:T(8,128)} %get-tuple-element.5.tgt_in), custom_call_target="tpu_custom_call" | custom-call | tf_op jit(solution)/shard_map/pallas_call | solution.py:220
